TPU v7x, 256 devices: a whole 4x4x8 slice. The times are simulated.
256 devices in a mesh: grp: 2 (over core), mr: 16 (over y_lo, z), mc: 8 (over y_hi, x).
Axes of the slice: x: 4, y: 4 (y_hi: 2, y_lo: 2; y = y_hi * 2 + y_lo), z: 8, core: 2. Of those that a mesh axis runs over, the one named last changes fastest.
Arguments:
- queries: bfloat16 [768, 8192], P(('grp', 'mr'), 'mc'), may hold values from -6 to 6
- new_keys: bfloat16 [768, 1024], P(('grp', 'mr'), 'mc'), may hold values from -6 to 6
- new_values: bfloat16 [768, 1024], P(('grp', 'mr'), 'mc'), may hold values from -6 to 6
- key_cache: bfloat16 [768, 512, 1024], P(('grp', 'mr'), None, 'mc'), may hold values from -6 to 6
- value_cache: bfloat16 [768, 512, 1024], P(('grp', 'mr'), None, 'mc'), may hold values from -6 to 6
- context_len: int32 [768], P(('grp', 'mr')), may hold values from 2 to 512, as said below
- cache_slot: int32 [768], P(('grp', 'mr')), may hold values from 0 to 767, as said below
- residual_in: bfloat16 [768, 8192], P(('grp', 'mr'), 'mc'), may hold values from -31 to 31
- out_weight: bfloat16 [8192, 8192], P(('grp', 'mr'), 'mc'), may hold values from -0.25 to 0.25
- gate_weight: bfloat16 [8192, 28672], P('mc', ('grp', 'mr')), may hold values from -0.0625 to 0.0625
- up_weight: bfloat16 [8192, 28672], P('mc', ('grp', 'mr')), may hold values from -0.0625 to 0.0625
Outputs:
- residual_out: bfloat16 [768, 8192], P(('grp', 'mr'), 'mc')
- activation: bfloat16 [768, 28672], P('mc', ('grp', 'mr'))
Inputs may be any that keep to these rules, and one draw needn't show every extreme that they name: Row r's history fills positions 0 to context_len[r] - 1 of its cache row; some row has 512. `cache_slot`: within each aligned block of 24 rows the values are a permutation of that block's own row indices.
All inputs are finite; a program needn't handle non-finite values.
Results may differ from a plain program's by a relative error of at most 0.006.
Values may be sent and summed in bfloat16 or wider, within the bound.
No kernel may reach another device: no remote copies, remote signals or barrier semaphores. Data moves between devices by JAX's collectives and lax.ppermute only.
A program may use at most 64 MiB of HBM per device.

v0:
```python
import math

import jax
import jax.numpy as jnp
from jax import lax
from jax.sharding import PartitionSpec as P

D = 8192
HD = 128


norm_epsilon = 1e-05
masked_score = -1e30


def copy_for_each(shard, axis):
    devices = lax.axis_size(axis)
    return lax.all_to_all(
        jnp.broadcast_to(shard[None], (devices, *shard.shape)), axis, 0, 0, tiled=True
    )


def in_order(parts, dim):
    parts = jnp.moveaxis(parts, 0, dim)
    dims = parts.shape
    return parts.reshape(*dims[:dim], dims[dim] * dims[dim + 1], *dims[dim + 2 :])


def collect(shard, axis, dim):
    parts = copy_for_each(shard, axis)
    return in_order(parts, dim)


def side_by_side(arrays, axis, dim, along):
    widths = [math.prod(a.shape[along:]) for a in arrays]
    both = jnp.concatenate(
        [a.reshape(*a.shape[:along], w) for a, w in zip(arrays, widths)], axis=along
    )
    filled = lax.psum_scatter(both, axis, scatter_dimension=dim, tiled=True)
    parts = jnp.split(filled, [sum(widths[:k]) for k in range(1, len(widths))], axis=along)
    return tuple(
        (b.reshape(*filled.shape[:along], *a.shape[along:]) for a, b in zip(arrays, parts))
    )


def attend_rows(queries, new_keys, new_values, key_rows, value_rows, context_len):
    row_denominator_sum = queries.shape[0]
    context = key_rows.shape[1]
    kv_heads = key_rows.shape[2] // HD
    groups = queries.shape[1] // key_rows.shape[2]
    attention_logit_scale = HD ** (-0.5)
    query_grouped_four = queries.reshape(row_denominator_sum, kv_heads, groups, HD)
    key_four = key_rows.reshape(row_denominator_sum, context, kv_heads, HD)
    value_four = value_rows.reshape(row_denominator_sum, context, kv_heads, HD)
    current_key = new_keys.reshape(row_denominator_sum, kv_heads, HD)
    own_value = new_values.reshape(row_denominator_sum, kv_heads, HD).astype(jnp.float32)
    scores = (
        jnp.einsum(
            "bkgd,bckd->bkgc", query_grouped_four, key_four, preferred_element_type=jnp.float32
        )
        * attention_logit_scale
    )
    positions = jnp.arange(context, dtype=jnp.int32)
    valid_mask = positions[None, :] < context_len[:, None]
    scores = jnp.where(valid_mask[:, None, None, :], scores, masked_score)
    current_score = (
        jnp.einsum(
            "cnhz,cnz->cnh", query_grouped_four, current_key, preferred_element_type=jnp.float32
        )
        * attention_logit_scale
    )
    row_max = jnp.maximum(jnp.max(scores, axis=3), current_score)
    exponent = jnp.exp(scores - row_max[..., None])
    own_exponent = jnp.exp(current_score - row_max)
    denominator = jnp.sum(exponent, axis=3) + own_exponent
    weights = (exponent / denominator[..., None]).astype(jnp.bfloat16)
    own_weight = (own_exponent / denominator).astype(jnp.bfloat16).astype(jnp.float32)
    combined = jnp.einsum(
        "bkgc,bckd->bkgd", weights, value_four, preferred_element_type=jnp.float32
    )
    combined = combined + own_weight[..., None] * own_value[:, :, None, :]
    return combined.reshape(row_denominator_sum, -1).astype(jnp.bfloat16)


def body(
    queries,
    new_keys,
    new_values,
    key_cache,
    value_cache,
    context_len,
    cache_slot,
    residual_in,
    out_weight,
    gate_weight,
    up_weight,
):
    local_rows = queries.shape[0]
    row_base = lax.axis_index(("grp", "mr")) * local_rows
    device_slot_index = cache_slot - row_base
    positions = jnp.arange(local_rows, dtype=jnp.int32)
    matches = device_slot_index[:, None] == positions[None, :]
    inverse = jnp.sum(jnp.where(matches, positions[:, None], 0), axis=0)
    by_cache = attend_rows(
        jnp.take(queries, inverse, axis=0),
        jnp.take(new_keys, inverse, axis=0),
        jnp.take(new_values, inverse, axis=0),
        key_cache,
        value_cache,
        jnp.take(context_len, inverse, axis=0),
    )
    attended = jnp.take(by_cache, device_slot_index, axis=0)
    gathered = collect(attended, "mc", 1)
    features = lax.all_to_all(gathered, ("grp", "mr"), split_axis=1, concat_axis=0, tiled=True)
    partial_value = jnp.dot(features, out_weight, preferred_element_type=jnp.float32)
    own_rows = lax.dynamic_slice_in_dim(partial_value, row_base, local_rows) + residual_in.astype(
        jnp.float32
    )
    partial_value = lax.dynamic_update_slice_in_dim(partial_value, own_rows, row_base, 0)
    summed = lax.psum(partial_value, ("grp", "mr"))
    everyone = summed.astype(jnp.bfloat16)
    residual_out = lax.dynamic_slice_in_dim(everyone, row_base, local_rows)
    widened = lax.optimization_barrier(everyone).astype(jnp.float32)
    squares = jnp.sum(widened * widened, axis=1)
    gate_term = jnp.dot(everyone, gate_weight, preferred_element_type=jnp.float32)
    up_term = jnp.dot(everyone, up_weight, preferred_element_type=jnp.float32)
    gate_sum, up_sum, square_sum = side_by_side((gate_term, up_term, squares), "mc", 0, 1)
    inverse_rms = lax.rsqrt(square_sum / D + norm_epsilon)
    gate_value = gate_sum * inverse_rms[:, None]
    upward = up_sum * inverse_rms[:, None]
    activation = (jax.nn.silu(gate_value) * upward).astype(jnp.bfloat16)
    return (residual_out, activation)


def solution(mesh):
    in_specs = (
        P(("grp", "mr"), "mc"),
        P(("grp", "mr"), "mc"),
        P(("grp", "mr"), "mc"),
        P(("grp", "mr"), None, "mc"),
        P(("grp", "mr"), None, "mc"),
        P(("grp", "mr")),
        P(("grp", "mr")),
        P(("grp", "mr"), "mc"),
        P(("grp", "mr"), "mc"),
        P("mc", ("grp", "mr")),
        P("mc", ("grp", "mr")),
    )
    out_specs = (P(("grp", "mr"), "mc"), P("mc", ("grp", "mr")))
    return jax.shard_map(body, mesh=mesh, in_specs=in_specs, out_specs=out_specs, check_vma=False)
```

profile of v0, /device:TPU:1, one launch (start us, length us, event | category | flops | bytes accessed | tf_op | source)
XLA Modules:
  0.0 330.5 jit_solution(5667355430699239794)
XLA Ops:
  7.2 0.0 copy-start
  7.2 0.8 compare_and_fusion
  8.0 0.1 select_reduce_fusion
  8.1 1.4 gather_fusion
  9.5 1.3 gather_fusion.3
  10.8 1.3 gather_fusion.2
  12.1 0.1 iota_compare_fusion
  12.1 1.4 gather_fusion.1
  13.6 0.0 copy-start.2
  13.6 0.1 select_bitcast_fusion
  13.7 0.1 select_convert_fusion
  13.8 0.1 fusion.10
  13.9 0.0 copy-done
  13.9 1.0 fusion.15
  14.9 0.2 fusion.2
  15.2 0.3 copy-done.2
  15.5 0.6 fusion.1
  16.1 0.6 gather_fusion.4
  16.7 0.1 broadcast_select_fusion
  16.8 16.8 %all_to_all.24 = bf16[8,24,1024]{2,1,0:T(8,128)(2,1)S(1)} all-to-all(bf16[8,24,1024]{2,1,0:T(8,128)(2,1)S(1)} %broadcast_in_dim.66), channel_id=1, replica_groups=mesh['grp'=2,'mr'=16,'mc'=8] {'mc'}, dimensions={0} | all-to-all | bytes 786432 | tf_op jit(solution)/shard_map/all_to_all | solution.py:18
  33.6 0.2 copy.18
  33.9 1.0 all_to_all.18
  34.8 2.0 copy.19
  36.8 10.3 %all-to-all-start.1 = ((bf16[24,32,256]{2,0,1:T(8,128)(2,1)}), bf16[24,32,256]{2,0,1:T(8,128)(2,1)S(1)}, u32[]{:S(2)}, u32[]{:S(2)}) async-start(bf16[24,32,256]{2,0,1:T(8,128)(2,1)} %copy.19), calls=%async_computation.1 | async-start | bytes 786432 | tf_op jit(solution)/shard_map/all_to_all | solution.py:114
  47.1 0.0 reduce-scatter.2.cloned.1.call-start
  47.2 13.3 %all-to-all-done.1 = bf16[24,32,256]{2,0,1:T(8,128)(2,1)S(1)} async-done(((bf16[24,32,256]{2,0,1:T(8,128)(2,1)}), bf16[24,32,256]{2,0,1:T(8,128)(2,1)S(1)}, u32[]{:S(2)}, u32[]{:S(2)}) %all-to-all-start.1) | async-done | bytes 393248 | tf_op jit(solution)/shard_map/all_to_all | solution.py:114
  60.5 0.0 copy-start.3
  60.5 3.3 fusion.16
  63.8 0.0 copy-done.3
  63.8 1.5 add_dynamic-update-slice_fusion
  65.3 145.9 %all-reduce.1 = bf16[768,1024]{1,0:T(8,128)(2,1)} all-reduce(f32[768,1024]{1,0:T(8,128)} %add_dynamic-update-slice_fusion), channel_id=1, replica_groups=mesh['grp'=2,'mr'=16,'mc'=8] {'grp','mr'}, use_global_device_ids=true, to_apply=%region_3.6 | all-reduce | flops 786432 | bytes 4718592 | tf_op jit(solution)/shard_map/psum | solution.py:120
  211.2 1.8 multiply_reduce_fusion
  213.0 0.2 reshape.190
  213.2 0.0 copy-start.1
  213.2 0.0 copy-start.4
  213.2 3.9 %fusion.18 = f32[768,896]{1,0:T(8,128)S(1)} fusion(bf16[768,1024]{1,0:T(8,128)(2,1)} %all-reduce.1, bf16[1024,896]{1,0:T(8,128)(2,1)} %param.25), kind=kOutput, calls=%fused_computation.55 | convolution fusion | flops 1409286144 | bytes 6160384 | tf_op jit(solution)/shard_map/dot_general | solution.py:126
  217.1 0.0 copy-done.1
  217.1 0.0 copy-done.4
  217.1 1.8 fusion.17
  218.9 2.9 pad_maximum_fusion
  221.8 0.0 reduce-scatter.2.cloned.1.call-update
  221.8 1.4 constant_dynamic-slice_fusion
  223.2 97.5 %reduce-scatter.2.cloned.1.call-done = f32[96,1793]{1,0:T(8,128)} async-done(((f32[768,1793]{1,0:T(8,128)}), f32[96,1793]{1,0:T(8,128)}) %reduce-scatter.2.cloned.1.call-update) | async-done | bytes 688528 | tf_op jit(solution)/shard_map/reduce_scatter | solution.py:39
  320.8 0.9 fusion.9
  321.7 1.9 fusion.4
  (10 shorter events, 0.1 us)
Async XLA Ops:
  7.2 6.7 %copy-start = (bf16[24,512,128]{2,1,0:T(8,128)(2,1)S(1)}, bf16[24,512,128]{2,1,0:T(8,128)(2,1)}, u32[]{:S(2)}) copy-start(bf16[24,512,128]{2,1,0:T(8,128)(2,1)} %param.18) | copy-start | bytes 9437188
  13.6 1.9 copy-start.2
  36.8 23.7 %all-to-all-start.1 = ((bf16[24,32,256]{2,0,1:T(8,128)(2,1)}), bf16[24,32,256]{2,0,1:T(8,128)(2,1)S(1)}, u32[]{:S(2)}, u32[]{:S(2)}) async-start(bf16[24,32,256]{2,0,1:T(8,128)(2,1)} %copy.19), calls=%async_computation.1 | async-start | bytes 786432 | tf_op jit(solution)/shard_map/all_to_all | solution.py:114
  47.1 273.6 %reduce-scatter.2.cloned.1.call-start = ((), (), s32[]{:S(2)}) async-start(), calls=%async_computation.3 | async-start | bytes 6635520 | tf_op jit(solution)/shard_map/reduce_scatter | solution.py:39
  60.5 3.3 copy-start.3
  213.2 3.9 %copy-start.1 = (bf16[768,1024]{1,0:T(8,128)(2,1)S(1)}, bf16[768,1024]{1,0:T(8,128)(2,1)}, u32[]{:S(2)}) copy-start(bf16[768,1024]{1,0:T(8,128)(2,1)} %all-reduce.1) | copy-start | bytes 4718596
  213.2 3.9 %copy-start.4 = (bf16[1024,896]{1,0:T(8,128)(2,1)S(1)}, bf16[1024,896]{1,0:T(8,128)(2,1)}, u32[]{:S(2)}) copy-start(bf16[1024,896]{1,0:T(8,128)(2,1)} %param.24) | copy-start | bytes 5505028
Sparse Core Ops, SparseCore 0:
  221.9 98.8 reduce-scatter.1
where the time goes:
time: 331 us; the launch traced here: 330 us
  blocking collectives  163 us (49%)
  waiting for transfers between devices  111 us (34%)
  between operations  14.2 us (4%)
  local copies, waits for them, and re-layouts  11.1 us (3%)
  matrix products  10.7 us (3%)
  other arithmetic  10.5 us (3%)
  starting transfers between devices  10.4 us (3%)
    psum x1, blocking collectives, body(): summed = lax.psum(partial_value, ('grp', 'mr'))  146 us
    reduce_scatter x1, waiting for transfers between devices, side_by_side(): filled = lax.psum_scatter(both, axis, scatter_dimension=dim, tiled=True)  97.5 us
    all_to_all x1, blocking collectives, copy_for_each(): lax.all_to_all(jnp.broadcast_to(shard[None], (devices, *shard.shape)), ax...  16.8 us
    all_to_all x1, waiting for transfers between devices, body(): lax.all_to_all(gathered, ('grp', 'mr'), split_axis=1, concat_axis=0, tile...  13.3 us
    all_to_all x1, starting transfers between devices, body(): lax.all_to_all(gathered, ('grp', 'mr'), split_axis=1, concat_axis=0, tile...  10.3 us
  transfers between devices with their start and end apart: 2, of which 2 were waited for; matrix products, arithmetic and copies ran while one was open for 0% of the time, Pallas kernels for 0%

commit v1 on v0

v1 whole, which is shorter than its diff:
```python
import functools
import itertools

import jax
import jax.numpy as jnp
from jax import lax
from jax.experimental import pallas as pl
from jax.experimental.pallas import tpu as pltpu
from jax.sharding import Mesh
from jax.sharding import PartitionSpec as P

D = 8192
HD = 128
EPS = 1e-05
MASKED = -1e30
BF = jnp.bfloat16
F32 = jnp.float32

FINE = ("g", "yl", "zh", "z1", "z0", "yh", "xh", "xl")
MC = ("yh", "xh", "xl")
KAPPA = ("yl", "zh", "z1")
YLZ = ("yl", "zh", "z1", "z0")


def dot(a, b, contract):
    return lax.dot_general(a, b, ((contract[0], contract[1]), ((), ())), preferred_element_type=F32)


def attend_kernel(slot_ref, len_ref, bit_ref, q_ref, nk_ref, nv_ref, k_hbm, v_hbm, a_ref, b_ref,
                  kbuf, vbuf, score, own, weight, own_weight, mixed, ksem, vsem):
    rows, context = kbuf.shape[0], kbuf.shape[1]
    heads = q_ref.shape[1] // HD

    def k_copy(r):
        return pltpu.make_async_copy(k_hbm.at[slot_ref[r]], kbuf.at[r], ksem.at[r])

    def v_copy(r):
        return pltpu.make_async_copy(v_hbm.at[slot_ref[r]], vbuf.at[r], vsem.at[r])

    for r in range(rows):
        k_copy(r).start()
    for r in range(rows):
        v_copy(r).start()
    scale = HD ** (-0.5)
    q = q_ref[...].astype(F32)
    nk = nk_ref[...].astype(F32)
    nv = nv_ref[...].astype(F32)
    position = lax.broadcasted_iota(jnp.int32, (heads, context), 1)
    group = 6
    for base in range(0, rows, group):
        for r in range(base, base + group):
            k_copy(r).wait()
        for r in range(base, base + group):
            q8 = jnp.concatenate(
                [q[r : r + 1, h * HD : (h + 1) * HD] for h in range(heads)], axis=0
            )
            s = dot(q8.astype(BF), kbuf[r], ((1,), (1,))) * scale
            score[r * heads : (r + 1) * heads, :] = jnp.where(position < len_ref[r], s, MASKED)
            mine = jnp.sum(q8 * nk[r : r + 1, :], axis=1, keepdims=True) * scale
            own[r * heads : (r + 1) * heads, :] = jnp.broadcast_to(mine, (heads, HD))
    s = score[...]
    mine = own[:, 0:1]
    top = jnp.maximum(jnp.max(s, axis=1, keepdims=True), mine)
    e = jnp.exp(s - top)
    own_e = jnp.exp(mine - top)
    total = jnp.sum(e, axis=1, keepdims=True) + own_e
    weight[...] = (e / total).astype(BF).astype(F32)
    own_weight[...] = jnp.broadcast_to((own_e / total).astype(BF).astype(F32), own_weight.shape)
    for base in range(0, rows, group):
        for r in range(base, base + group):
            v_copy(r).wait()
        for r in range(base, base + group):
            w = weight[r * heads : (r + 1) * heads, :].astype(BF)
            o = dot(w, vbuf[r], ((1,), (0,)))
            mixed[r] = o + own_weight[r * heads : (r + 1) * heads, :] * nv[r : r + 1, :]
    half_bit, quarter_bit = bit_ref[0], bit_ref[1]
    out = mixed[...]
    for h in range(heads):
        half, quarter, inner = h // 4, (h // 2) % 2, h % 2
        value = out[:, h, :].astype(BF)
        lanes = slice(inner * HD, (inner + 1) * HD)

        @pl.when(half == half_bit)
        def _(value=value, quarter=quarter, lanes=lanes):
            a_ref[jnp.bitwise_xor(quarter, quarter_bit), :, lanes] = value

        @pl.when(half != half_bit)
        def _(value=value, quarter=quarter, lanes=lanes):
            b_ref[jnp.bitwise_xor(quarter, quarter_bit), :, lanes] = value


def attend(slots, lens, bits, queries, new_keys, new_values, key_cache, value_cache):
    rows, context = key_cache.shape[0], key_cache.shape[1]
    heads = queries.shape[1] // HD
    smem = pl.BlockSpec(memory_space=pltpu.SMEM)
    vmem = pl.BlockSpec(memory_space=pltpu.VMEM)
    hbm = pl.BlockSpec(memory_space=pl.ANY)
    part = jax.ShapeDtypeStruct((2, rows, 2 * HD), BF)
    return pl.pallas_call(
        attend_kernel,
        out_shape=(part, part),
        in_specs=[smem, smem, smem, vmem, vmem, vmem, hbm, hbm],
        out_specs=(vmem, vmem),
        scratch_shapes=[
            pltpu.VMEM((rows, context, HD), BF),
            pltpu.VMEM((rows, context, HD), BF),
            pltpu.VMEM((rows * heads, context), F32),
            pltpu.VMEM((rows * heads, HD), F32),
            pltpu.VMEM((rows * heads, context), F32),
            pltpu.VMEM((rows * heads, HD), F32),
            pltpu.VMEM((rows, heads, HD), F32),
            pltpu.SemaphoreType.DMA((rows,)),
            pltpu.SemaphoreType.DMA((rows,)),
        ],
        compiler_params=pltpu.CompilerParams(vmem_limit_bytes=48 << 20),
        name="attend",
    )(slots, lens, bits, queries, new_keys, new_values, key_cache, value_cache)


def project_kernel(a_order, b_order, bit_ref, xa_ref, xb_ref, w00, w01, w10, w11, out_ref):
    parts, rows = out_ref.shape[0], out_ref.shape[1]

    def stack(ref, order, quarter):
        return jnp.concatenate([ref[order[p], quarter].astype(F32) for p in range(parts)], axis=0).astype(BF)

    swap = bit_ref[0]
    for first, second, when in ((( xa_ref, a_order), (xb_ref, b_order), 0), ((xb_ref, b_order), (xa_ref, a_order), 1)):
        @pl.when(swap == when)
        def _(first=first, second=second):
            total = dot(stack(*first, 0), w00[...], ((1,), (0,)))
            total += dot(stack(*first, 1), w01[...], ((1,), (0,)))
            total += dot(stack(*second, 0), w10[...], ((1,), (0,)))
            total += dot(stack(*second, 1), w11[...], ((1,), (0,)))
            out_ref[...] = total.reshape(parts, rows, total.shape[1]).astype(BF)


def project(bit, xa, xb, weights, a_order, b_order):
    parts, _, rows, _ = xa.shape
    vmem = pl.BlockSpec(memory_space=pltpu.VMEM)
    return pl.pallas_call(
        functools.partial(project_kernel, a_order, b_order),
        out_shape=jax.ShapeDtypeStruct((parts, rows, weights[0].shape[1]), BF),
        in_specs=[pl.BlockSpec(memory_space=pltpu.SMEM)] + [vmem] * 6,
        out_specs=vmem,
        compiler_params=pltpu.CompilerParams(vmem_limit_bytes=32 << 20),
        name="project",
    )(bit, xa, xb, *weights)


def join_kernel(parts_ref, residual_ref, out_ref, copies_ref):
    total = residual_ref[...].astype(F32)
    acc = parts_ref[0].astype(F32)
    for p in range(1, parts_ref.shape[0]):
        acc += parts_ref[p].astype(F32)
    total = (total + acc).astype(BF)
    out_ref[...] = total
    for c in range(copies_ref.shape[0]):
        copies_ref[c] = total


def join(parts, residual, copies):
    vmem = pl.BlockSpec(memory_space=pltpu.VMEM)
    return pl.pallas_call(
        join_kernel,
        out_shape=(
            jax.ShapeDtypeStruct(residual.shape, BF),
            jax.ShapeDtypeStruct((copies, *residual.shape), BF),
        ),
        in_specs=[vmem, vmem],
        out_specs=(vmem, vmem),
        name="join",
    )(parts, residual)


def expand_kernel(base_ref, x_ref, wg_ref, wu_ref, *rest):
    u_ref = rest[-2]
    held = rest[-1]
    c = pl.program_id(0)
    per_dest = held.shape[0] // 2

    @pl.when(c == 0)
    def _():
        x = x_ref[...].astype(F32)
        held[...] = x.reshape(held.shape).astype(BF)
        ones = jnp.ones((16, held.shape[1]), BF)
        for d in range(2):
            v = held[d * per_dest : (d + 1) * per_dest, :].astype(F32)
            square = v * v
            high = square.astype(BF)
            low = (square - high.astype(F32)).astype(BF)
            total = dot(ones, high, ((1,), (1,))) + dot(ones, low, ((1,), (1,)))
            upper = total.astype(BF).astype(F32)
            lower = total - upper
            line = lax.broadcasted_iota(jnp.int32, total.shape, 0)
            both = jnp.where(line == 0, upper, jnp.where(line == 1, lower, 0.0))
            tail = u_ref.shape[1] - 16
            u_ref[d, tail:, :] = jnp.zeros((16, HD), BF)
            u_ref[d, tail:, 0:per_dest] = both.astype(BF)

    w = jnp.concatenate([wg_ref[...], wu_ref[...]], axis=1)
    y = dot(held[...], w, ((1,), (0,))).astype(BF)
    start = pl.multiple_of(c * (2 * per_dest), 2 * per_dest)
    for d in range(2):
        mine = y[d * per_dest : (d + 1) * per_dest, :]
        u_ref[d, pl.ds(start, per_dest), :] = mine[:, :HD]
        u_ref[d, pl.ds(start + per_dest, per_dest), :] = mine[:, HD:]


def expand(base, x, wg, wu, so_far):
    parts, rows, depth = x.shape
    steps = wg.shape[1] // HD
    per_dest = parts * rows // 2
    height = steps * 2 * per_dest + 16
    specs = [
        pl.BlockSpec((parts, rows, depth), lambda c, base: (0, 0, 0)),
        pl.BlockSpec((depth, HD), lambda c, base: (0, c)),
        pl.BlockSpec((depth, HD), lambda c, base: (0, c)),
    ]
    args = [x, wg, wu]
    aliases = {}
    if so_far is not None:
        specs.append(pl.BlockSpec(memory_space=pl.ANY))
        args.append(so_far)
        aliases = {4: 0}
    return pl.pallas_call(
        expand_kernel,
        out_shape=jax.ShapeDtypeStruct((8, height, HD), BF),
        grid_spec=pltpu.PrefetchScalarGridSpec(
            num_scalar_prefetch=1,
            grid=(steps,),
            in_specs=specs,
            out_specs=pl.BlockSpec((2, height, HD), lambda c, base: (base[0], 0, 0)),
            scratch_shapes=[pltpu.VMEM((parts * rows, depth), BF)],
        ),
        input_output_aliases=aliases,
        compiler_params=pltpu.CompilerParams(vmem_limit_bytes=32 << 20),
        name="expand",
    )(base, *args)


def activate_kernel(u_ref, square_ref, out_ref, scale):
    per_dest = out_ref.shape[0]

    @pl.when(pl.program_id(0) == 0)
    def _():
        s = square_ref[0].astype(F32)
        for p in range(1, square_ref.shape[0]):
            s += square_ref[p].astype(F32)
        line = s[0:1, :] + s[1:2, :]
        square = jnp.broadcast_to(line, (HD, HD)).T
        scale[...] = lax.rsqrt(square[:per_dest, :] / D + EPS)

    total = u_ref[0].astype(F32)
    for p in range(1, u_ref.shape[0]):
        total += u_ref[p].astype(F32)
    gate = total[:per_dest] * scale[...]
    up = total[per_dest:] * scale[...]
    out_ref[...] = (gate / (1.0 + jnp.exp(-gate)) * up).astype(BF)


def activate(u, per_dest, columns):
    parts, height, _ = u.shape
    steps = columns // HD
    return pl.pallas_call(
        activate_kernel,
        out_shape=jax.ShapeDtypeStruct((per_dest, columns), BF),
        grid=(steps,),
        in_specs=[
            pl.BlockSpec((parts, 2 * per_dest, HD), lambda c: (0, c, 0)),
            pl.BlockSpec((parts, 16, HD), lambda c: (0, (height - 16) // 16, 0)),
        ],
        out_specs=pl.BlockSpec((per_dest, HD), lambda c: (0, c)),
        scratch_shapes=[pltpu.VMEM((per_dest, HD), F32)],
        name="activate",
    )(u, u)


def number(*bits):
    n = 0
    for b in bits:
        n = 2 * n + b
    return n


def partner_pairs(which):
    pairs = []
    for g, z0, a, b, c, d, e, f in itertools.product(range(2), repeat=8):
        half = d if which == 0 else 1 - d
        first = c if which == 0 else 1 - c
        pairs.append((number(g, a, b, c, z0, d, e, f), number(g, e, f, half, z0, first, a, b)))
    return pairs


def source_order(which):
    order = []
    for a, b, c in itertools.product(range(2), repeat=3):
        order.append(number(c if which == 0 else 1 - c, a, b))
    return tuple(order)


def swapped(x, axis):
    return lax.ppermute(x, axis, [(0, 1), (1, 0)])


def exchange(x, axes):
    return lax.all_to_all(x, axes, 0, 0, tiled=True)


def scalar(*values):
    return jnp.stack([jnp.asarray(v, jnp.int32) for v in values])


def body(queries, new_keys, new_values, key_cache, value_cache, context_len, cache_slot,
         residual_in, out_weight, gate_weight, up_weight):
    rows = queries.shape[0]
    g, yl, z1, z0, yh = (lax.axis_index(a) for a in ("g", "yl", "z1", "z0", "yh"))
    row_base = lax.axis_index(("g",) + YLZ) * rows

    w00 = out_weight
    w01 = swapped(out_weight, "z0")
    w10 = swapped(out_weight, "g")
    w11 = swapped(w01, "g")

    half_a, half_b = attend(cache_slot - row_base, context_len, scalar(yh, z0), queries, new_keys,
                            new_values, key_cache, value_cache)
    half_a = lax.ppermute(half_a, FINE, partner_pairs(0))
    half_b = lax.ppermute(half_b, FINE, partner_pairs(1))
    both = jnp.stack([half_a, half_b])
    spread = exchange(jnp.broadcast_to(both[None], (8, *both.shape)), MC)
    partial = project(scalar(jnp.bitwise_xor(g, z1)), spread[:, 0], spread[:, 1], (w00, w01, w10, w11),
                      source_order(0), source_order(1))
    residual_out, copies = join(exchange(partial, KAPPA), residual_in, 16)
    everyone = exchange(copies, YLZ)
    mine, theirs = everyone, swapped(everyone, "g")
    u = None
    for block, gg in ((mine, g), (theirs, 1 - g)):
        for part in range(2):
            u = expand(scalar(gg * 2 + part), block[8 * part : 8 * part + 8], gate_weight, up_weight, u)
    activation = activate(exchange(u, MC), 4 * rows, gate_weight.shape[1])
    return (residual_out, activation)


def solution(mesh):
    fine = Mesh(mesh.devices.reshape((2,) * 8), FINE)
    r = ("g",) + YLZ
    in_specs = (P(r, MC), P(r, MC), P(r, MC), P(r, None, MC), P(r, None, MC), P(r), P(r), P(r, MC),
                P(r, MC), P(MC, r), P(MC, r))
    out_specs = (P(r, MC), P(MC, r))
    return jax.shard_map(body, mesh=fine, in_specs=in_specs, out_specs=out_specs, check_vma=False)
```

time: 331 us -> 153 us (0.46)
  waiting for transfers between devices: 111 us -> 6.69 us
  blocking collectives: 163 us -> 73.5 us
  Pallas kernels: 0 us -> 28 us
  starting transfers between devices: 10.4 us -> 35.8 us
  between operations: 14.2 us -> 0.78 us
  matrix products: 10.7 us -> 0 us
  other arithmetic: 10.5 us -> 0.74 us
  local copies, waits for them, and re-layouts: 11.1 us -> 7.14 us
    psum x1 -> x0, blocking collectives: 146 us -> none  [body(): summed = lax.psum(partial_value, ('grp', 'mr'))]
    reduce_scatter x1 -> x0, waiting for transfers between devices: 97.5 us -> none  [side_by_side(): filled = lax.psum_scatter(both, axis, scatter_dimension=dim, tiled=True)]
    all_to_all x1 -> x3, blocking collectives: 16.8 us -> 73.5 us  [exchange(): return lax.all_to_all(x, axes, 0, 0, tiled=True)]
    pallas_call x0 -> x8, Pallas kernels: none -> 28 us  [the longest x4 12.2 us: expand(): pl.pallas_call(expand_kernel, out_shape=jax.ShapeDtypeStruct((8, height,...]
    ppermute x0 -> x6, starting transfers between devices: none -> 20.5 us  [the longest x4 12.3 us: swapped(): return lax.ppermute(x, axis, [(0, 1), (1, 0)])]
    dot_general x6 -> x0, matrix products: 10.7 us -> none  [the longest x1 3.9 us: body(): up_term = jnp.dot(everyone, up_weight, preferred_element_type=jnp.float32)]
    all_to_all x1, waiting for transfers between devices: 13.3 us -> 5.47 us  [exchange(): return lax.all_to_all(x, axes, 0, 0, tiled=True)]
    gather x5 -> x0, local copies, waits for them, and re-layouts: 5.96 us -> none  [the longest x1 1.45 us: body(): jnp.take(queries, inverse, axis=0)]
  transfers between devices with their start and end apart: 2 -> 7, of which waited for: 2 -> 2; matrix products, arithmetic and copies ran while one was open for 0% -> 1% of each run, Pallas kernels for 0% -> 9%
where the time goes in v1:
time: 153 us
  blocking collectives  73.5 us (48%)
  starting transfers between devices  35.8 us (23%)
  Pallas kernels  28 us (18%)
  local copies, waits for them, and re-layouts  7.14 us (5%)
  waiting for transfers between devices  6.69 us (4%)
    all_to_all x3, blocking collectives, exchange(): return lax.all_to_all(x, axes, 0, 0, tiled=True)  73.5 us
    all_to_all x1, starting transfers between devices, exchange(): return lax.all_to_all(x, axes, 0, 0, tiled=True)  15.3 us
    ppermute x4, starting transfers between devices, swapped(): return lax.ppermute(x, axis, [(0, 1), (1, 0)])  12.3 us
    pallas_call x4, Pallas kernels, expand(): pl.pallas_call(expand_kernel, out_shape=jax.ShapeDtypeStruct((8, height,...  12.2 us
    pallas_call x1, Pallas kernels, attend(): pl.pallas_call(attend_kernel, out_shape=(part, part), in_specs=[smem, sme...  7.89 us
    ppermute x1, starting transfers between devices, body(): half_b = lax.ppermute(half_b, FINE, partner_pairs(1))  7.54 us
    unnamed x16, local copies, waits for them, and re-layouts  6.23 us
    all_to_all x1, waiting for transfers between devices, exchange(): return lax.all_to_all(x, axes, 0, 0, tiled=True)  5.47 us
  transfers between devices with their start and end apart: 7, of which 2 were waited for; matrix products, arithmetic and copies ran while one was open for 1% of the time, Pallas kernels for 9%

profile of v1, /device:TPU:1, one launch (start us, length us, event | category | flops | bytes accessed | tf_op | source)
XLA Modules:
  0.0 152.6 jit_solution(8625103201875915088)
XLA Ops:
  0.6 2.6 %collective-permute-start.2 = (bf16[256,1024]{1,0:T(8,128)(2,1)}, bf16[256,1024]{1,0:T(8,128)(2,1)S(1)}, u32[]{:S(2)}, u32[]{:S(2)}) collective-permute-start(bf16[256,1024]{1,0:T(8,128)(2,1)} %w00.1), channel_id=1, source_target_pairs={{0,8},{8,0},{1,9},{9,1},{2,10},{10,2},{3,11},{11,3},{4,12},{12,4},... | collective-permute-start | bytes 1572872 | tf_op jit(solution)/shard_map/ppermute | solution.py:302
  3.2 0.1 pad_add_fusion.bit_ref
  3.3 0.7 broadcast_subtract_fusion.slot_ref
  3.9 0.0 copy-start.2
  3.9 1.9 %copy-done.2 = bf16[24,512,128]{2,1,0:T(8,128)(2,1)S(1)} copy-done((bf16[24,512,128]{2,1,0:T(8,128)(2,1)S(1)}, bf16[24,512,128]{2,1,0:T(8,128)(2,1)}, u32[]{:S(2)}) %copy-start.2) | copy-done | bytes 3145752
  5.8 0.0 copy-start.4
  5.8 0.8 copy-done.4
  6.6 0.0 copy-start.5
  6.6 0.7 copy-done.5
  7.3 0.0 copy-start.6
  7.3 0.7 copy-done.6
  8.0 0.0 copy-start.7
  8.0 0.7 copy-done.7
  8.6 0.0 copy-start.3
  8.6 7.9 %attend.1 = (bf16[2,24,256]{2,1,0:T(8,128)(2,1)S(1)}, bf16[2,24,256]{2,1,0:T(8,128)(2,1)S(1)}) custom-call(s32[24]{0:T(128)S(1)} %broadcast_subtract_fusion.slot_ref, s32[24]{0:T(128)S(1)} %copy-done.7, s32[2]{0:T(128)S(1)} %pad_add_fusion.bit_ref, bf16[24,1024]{1,0:T(8,128)(2,1)S(1)} %copy-done.4, bf16[24,128]{1,0:T(8,128)(2,1)S(1)} %copy-done.5, ...), custom_call_target="tpu_custom_call" | custom-call | tf_op jit(solution)/shard_map/attend/pallas_call | solution.py:99
  16.5 0.7 collective-permute-start
  17.2 7.5 %collective-permute-start.1 = (bf16[2,24,256]{2,1,0:T(8,128)(2,1)S(1)}, bf16[2,24,256]{2,1,0:T(8,128)(2,1)S(1)}, u32[]{:S(2)}, u32[]{:S(2)}) collective-permute-start(bf16[2,24,256]{2,1,0:T(8,128)(2,1)S(1)} %get-tuple-element.7), channel_id=1, source_target_pairs={{0,20},{1,52},{2,84},{3,116},{4,4},{5,36},{6,68},{7,100},{16,16},{... | collective-permute-start | bytes 73736 | tf_op jit(solution)/shard_map/ppermute | solution.py:327
  24.8 0.0 collective-permute-done
  24.8 1.2 collective-permute-done.1
  26.0 0.8 broadcast_in_dim.2
  26.8 15.3 %all-to-all-start = ((bf16[8,2,2,24,256]{4,3,2,1,0:T(8,128)(2,1)}), bf16[8,2,2,24,256]{4,3,2,1,0:T(8,128)(2,1)S(1)}, u32[]{:S(2)}, u32[]{:S(2)}) async-start(bf16[8,2,2,24,256]{4,3,2,1,0:T(8,128)(2,1)} %broadcast_in_dim.2), calls=%async_computation | async-start | bytes 786432 | tf_op jit(solution)/shard_map/all_to_all | solution.py:306
  42.1 0.0 copy-done.3
  42.1 2.8 %collective-permute-start.3 = (bf16[256,1024]{1,0:T(8,128)(2,1)S(1)}, bf16[256,1024]{1,0:T(8,128)(2,1)S(1)}, u32[]{:S(2)}, u32[]{:S(2)}) collective-permute-start(bf16[256,1024]{1,0:T(8,128)(2,1)S(1)} %copy-done.3), channel_id=1, source_target_pairs={{0,128},{128,0},{1,129},{129,1},{2,130},{130,2},{3,131},{131,3},{4... | collective-permute-start | bytes 1572872 | tf_op jit(solution)/shard_map/ppermute | solution.py:302
  44.8 0.0 collective-permute-done.2.w01
  44.8 0.1 collective-permute-start.4
  44.9 5.5 %all-to-all-done = bf16[8,2,2,24,256]{4,3,2,1,0:T(8,128)(2,1)S(1)} async-done(((bf16[8,2,2,24,256]{4,3,2,1,0:T(8,128)(2,1)}), bf16[8,2,2,24,256]{4,3,2,1,0:T(8,128)(2,1)S(1)}, u32[]{:S(2)}, u32[]{:S(2)}) %all-to-all-start) | async-done | bytes 393248 | tf_op jit(solution)/shard_map/all_to_all | solution.py:306
  50.4 0.0 collective-permute-done.3.w10
  50.4 0.0 collective-permute-done.4.w11
  50.4 0.6 project.1
  51.1 0.0 copy-start
  51.1 13.7 %all_to_all.20.parts_ref = bf16[8,24,1024]{2,1,0:T(8,128)(2,1)} all-to-all(bf16[8,24,1024]{2,1,0:T(8,128)(2,1)S(1)} %project.1), channel_id=1, replica_groups=mesh['g'=2,'yl'=2,'zh'=2,'z1'=2,'z0'=2,'yh'=2,'xh'=2,'xl'=2] {'yl','zh',..., dimensions={0} | all-to-all | bytes 786432 | tf_op jit(solution)/shard_map/all_to_all | solution.py:306
  64.8 2.0 %join.1 = (bf16[24,1024]{1,0:T(8,128)(2,1)}, bf16[16,24,1024]{2,1,0:T(8,128)(2,1)}) custom-call(bf16[8,24,1024]{2,1,0:T(8,128)(2,1)} %all_to_all.20.parts_ref, bf16[24,1024]{1,0:T(8,128)(2,1)} %residual_ref.1), custom_call_target="tpu_custom_call" | custom-call | tf_op jit(solution)/shard_map/join/pallas_call | solution.py:163
  66.8 19.1 %all_to_all.21 = bf16[16,24,1024]{2,1,0:T(8,128)(2,1)S(1)} all-to-all(bf16[16,24,1024]{2,1,0:T(8,128)(2,1)} %get-tuple-element.9), channel_id=1, replica_groups=mesh['g'=2,'yl'=2,'zh'=2,'z1'=2,'z0'=2,'yh'=2,'xh'=2,'xl'=2] {'yl','zh',..., dimensions={0} | all-to-all | bytes 1572864 | tf_op jit(solution)/shard_map/all_to_all | solution.py:306
  85.9 6.9 %collective-permute-start.5 = (bf16[16,24,1024]{2,1,0:T(8,128)(2,1)S(1)}, bf16[16,24,1024]{2,1,0:T(8,128)(2,1)S(1)}, u32[]{:S(2)}, u32[]{:S(2)}) collective-permute-start(bf16[16,24,1024]{2,1,0:T(8,128)(2,1)S(1)} %all_to_all.21), channel_id=1, source_target_pairs={{0,128},{128,0},{1,129},{129,1},{2,130},{130,2},{3,131},{131,3},{4... | collective-permute-start | bytes 2359304 | tf_op jit(solution)/shard_map/ppermute | solution.py:302
  92.8 0.1 fusion
  92.8 0.0 copy-done
  92.8 0.0 copy-start.1
  92.9 1.5 copy-done.1
  94.3 3.0 %expand.4.rest_0_ = bf16[8,1360,128]{2,1,0:T(8,128)(2,1)S(1)} custom-call(s32[1]{0:T(128)} %bitcast.10.base_ref, bf16[8,24,1024]{2,1,0:T(8,128)(2,1)S(1)} %get-tuple-element.10.x_ref, bf16[1024,896]{1,0:T(8,128)(2,1)S(1)} %copy-done, bf16[1024,896]{1,0:T(8,128)(2,1)S(1)} %copy-done.1), custom_call_target="tpu_custom_call" | custom-call | tf_op jit(solution)/shard_map/expand/pallas_call | solution.py:225
  97.4 3.1 %expand.5.rest_0_ = bf16[8,1360,128]{2,1,0:T(8,128)(2,1)S(1)} custom-call(s32[1]{0:T(128)} %bitcast.9.base_ref, bf16[8,24,1024]{2,1,0:T(8,128)(2,1)S(1)} %get-tuple-element.11.x_ref, bf16[1024,896]{1,0:T(8,128)(2,1)S(1)} %copy-done, bf16[1024,896]{1,0:T(8,128)(2,1)S(1)} %copy-done.1, ...), custom_call_target="tpu_custom_call", output_to_operand_aliasing={{}: (4, {})} | custom-call | tf_op jit(solution)/shard_map/expand/pallas_call | solution.py:225
  100.5 0.0 collective-permute-done.5
  100.5 0.1 fusion.1
  100.6 3.1 %expand.6.rest_0_ = bf16[8,1360,128]{2,1,0:T(8,128)(2,1)S(1)} custom-call(s32[1]{0:T(128)} %bitcast.8.base_ref, bf16[8,24,1024]{2,1,0:T(8,128)(2,1)S(1)} %get-tuple-element.12.x_ref, bf16[1024,896]{1,0:T(8,128)(2,1)S(1)} %copy-done, bf16[1024,896]{1,0:T(8,128)(2,1)S(1)} %copy-done.1, ...), custom_call_target="tpu_custom_call", output_to_operand_aliasing={{}: (4, {})} | custom-call | tf_op jit(solution)/shard_map/expand/pallas_call | solution.py:225
  103.6 3.1 %expand.7 = bf16[8,1360,128]{2,1,0:T(8,128)(2,1)S(1)} custom-call(s32[1]{0:T(128)} %bitcast.7.base_ref, bf16[8,24,1024]{2,1,0:T(8,128)(2,1)S(1)} %get-tuple-element.13.x_ref, bf16[1024,896]{1,0:T(8,128)(2,1)S(1)} %copy-done, bf16[1024,896]{1,0:T(8,128)(2,1)S(1)} %copy-done.1, bf16[8,1360,128]{2,1,0:T(8,128)(2,1)S(1)} %expand.6.rest_0_), custom_call_target="tpu_custom_call", output_to_operand_aliasing={{}: (4, {})} | custom-call | tf_op jit(solution)/shard_map/expand/pallas_call | solution.py:225
  106.7 40.7 %all_to_all.22.u_ref.square_ref = bf16[8,1360,128]{2,1,0:T(8,128)(2,1)} all-to-all(bf16[8,1360,128]{2,1,0:T(8,128)(2,1)S(1)} %expand.7), channel_id=1, replica_groups=mesh['g'=2,'yl'=2,'zh'=2,'z1'=2,'z0'=2,'yh'=2,'xh'=2,'xl'=2] {'yh','xh',..., dimensions={0} | all-to-all | bytes 5570560 | tf_op jit(solution)/shard_map/all_to_all | solution.py:306
  147.4 5.2 %activate.1 = bf16[96,896]{1,0:T(8,128)(2,1)} custom-call(bf16[8,1360,128]{2,1,0:T(8,128)(2,1)} %all_to_all.22.u_ref.square_ref, bf16[8,1360,128]{2,1,0:T(8,128)(2,1)} %all_to_all.22.u_ref.square_ref), custom_call_target="tpu_custom_call" | custom-call | tf_op jit(solution)/shard_map/activate/pallas_call | solution.py:264
  (2 shorter events, 0.0 us)
Async XLA Ops:
  0.6 44.2 %collective-permute-start.2 = (bf16[256,1024]{1,0:T(8,128)(2,1)}, bf16[256,1024]{1,0:T(8,128)(2,1)S(1)}, u32[]{:S(2)}, u32[]{:S(2)}) collective-permute-start(bf16[256,1024]{1,0:T(8,128)(2,1)} %w00.1), channel_id=1, source_target_pairs={{0,8},{8,0},{1,9},{9,1},{2,10},{10,2},{3,11},{11,3},{4,12},{12,4},... | collective-permute-start | bytes 1572872 | tf_op jit(solution)/shard_map/ppermute | solution.py:302
  3.9 1.9 %copy-start.2 = (bf16[24,512,128]{2,1,0:T(8,128)(2,1)S(1)}, bf16[24,512,128]{2,1,0:T(8,128)(2,1)}, u32[]{:S(2)}) copy-start(bf16[24,512,128]{2,1,0:T(8,128)(2,1)} %k_hbm.1) | copy-start | bytes 9437188
  5.8 0.8 copy-start.4
  6.6 0.7 copy-start.5
  7.3 0.7 copy-start.6
  8.0 0.7 copy-start.7
  8.6 33.4 %copy-start.3 = (bf16[256,1024]{1,0:T(8,128)(2,1)S(1)}, bf16[256,1024]{1,0:T(8,128)(2,1)}, u32[]{:S(2)}) copy-start(bf16[256,1024]{1,0:T(8,128)(2,1)} %w00.1) | copy-start | bytes 1572868
  16.5 8.2 %collective-permute-start = (bf16[2,24,256]{2,1,0:T(8,128)(2,1)S(1)}, bf16[2,24,256]{2,1,0:T(8,128)(2,1)S(1)}, u32[]{:S(2)}, u32[]{:S(2)}) collective-permute-start(bf16[2,24,256]{2,1,0:T(8,128)(2,1)S(1)} %get-tuple-element.6), channel_id=1, source_target_pairs={{0,0},{1,32},{2,64},{3,96},{4,16},{5,48},{6,80},{7,112},{16,4},{17... | collective-permute-start | bytes 73736 | tf_op jit(solution)/shard_map/ppermute | solution.py:326
  17.2 8.8 %collective-permute-start.1 = (bf16[2,24,256]{2,1,0:T(8,128)(2,1)S(1)}, bf16[2,24,256]{2,1,0:T(8,128)(2,1)S(1)}, u32[]{:S(2)}, u32[]{:S(2)}) collective-permute-start(bf16[2,24,256]{2,1,0:T(8,128)(2,1)S(1)} %get-tuple-element.7), channel_id=1, source_target_pairs={{0,20},{1,52},{2,84},{3,116},{4,4},{5,36},{6,68},{7,100},{16,16},{... | collective-permute-start | bytes 73736 | tf_op jit(solution)/shard_map/ppermute | solution.py:327
  26.8 23.6 %all-to-all-start = ((bf16[8,2,2,24,256]{4,3,2,1,0:T(8,128)(2,1)}), bf16[8,2,2,24,256]{4,3,2,1,0:T(8,128)(2,1)S(1)}, u32[]{:S(2)}, u32[]{:S(2)}) async-start(bf16[8,2,2,24,256]{4,3,2,1,0:T(8,128)(2,1)} %broadcast_in_dim.2), calls=%async_computation | async-start | bytes 786432 | tf_op jit(solution)/shard_map/all_to_all | solution.py:306
  42.1 8.4 %collective-permute-start.3 = (bf16[256,1024]{1,0:T(8,128)(2,1)S(1)}, bf16[256,1024]{1,0:T(8,128)(2,1)S(1)}, u32[]{:S(2)}, u32[]{:S(2)}) collective-permute-start(bf16[256,1024]{1,0:T(8,128)(2,1)S(1)} %copy-done.3), channel_id=1, source_target_pairs={{0,128},{128,0},{1,129},{129,1},{2,130},{130,2},{3,131},{131,3},{4... | collective-permute-start | bytes 1572872 | tf_op jit(solution)/shard_map/ppermute | solution.py:302
  44.8 5.6 %collective-permute-start.4 = (bf16[256,1024]{1,0:T(8,128)(2,1)S(1)}, bf16[256,1024]{1,0:T(8,128)(2,1)S(1)}, u32[]{:S(2)}, u32[]{:S(2)}) collective-permute-start(bf16[256,1024]{1,0:T(8,128)(2,1)S(1)} %collective-permute-done.2.w01), channel_id=1, source_target_pairs={{0,128},{128,0},{1,129},{129,1},{2,130},{130,2},{3,131},{131,3},{4... | collective-permute-start | bytes 1572872 | tf_op jit(solution)/shard_map/ppermute | solution.py:302
  51.1 41.8 %copy-start = (bf16[1024,896]{1,0:T(8,128)(2,1)S(1)}, bf16[1024,896]{1,0:T(8,128)(2,1)}, u32[]{:S(2)}) copy-start(bf16[1024,896]{1,0:T(8,128)(2,1)} %wg_ref.7) | copy-start | bytes 5505028
  85.9 14.6 %collective-permute-start.5 = (bf16[16,24,1024]{2,1,0:T(8,128)(2,1)S(1)}, bf16[16,24,1024]{2,1,0:T(8,128)(2,1)S(1)}, u32[]{:S(2)}, u32[]{:S(2)}) collective-permute-start(bf16[16,24,1024]{2,1,0:T(8,128)(2,1)S(1)} %all_to_all.21), channel_id=1, source_target_pairs={{0,128},{128,0},{1,129},{129,1},{2,130},{130,2},{3,131},{131,3},{4... | collective-permute-start | bytes 2359304 | tf_op jit(solution)/shard_map/ppermute | solution.py:302
  92.8 1.5 copy-start.1

commit v2 on v1

v2 whole, which is shorter than its diff:
```python
import functools

import jax
import jax.numpy as jnp
from jax import lax
from jax.experimental import pallas as pl
from jax.experimental.pallas import tpu as pltpu
from jax.sharding import Mesh
from jax.sharding import PartitionSpec as P

D = 8192
HD = 128
EPS = 1e-05
MASKED = -1e30
BF = jnp.bfloat16
F32 = jnp.float32

FINE = ("g", "yl", "zh", "z1", "z0", "yh", "xh", "xl")
MC = ("yh", "xh", "xl")
KAPPA = ("yl", "zh", "z1")
YLZ = ("yl", "zh", "z1", "z0")


def dot(a, b, contract):
    return lax.dot_general(a, b, ((contract[0], contract[1]), ((), ())), preferred_element_type=F32)


def in_hbm(x):
    return pltpu.with_memory_space_constraint(x, pltpu.HBM)


def attend_kernel(slot_hbm, len_hbm, q_hbm, nk_hbm, nv_hbm, k_hbm, v_hbm, out_ref,
                  slot, length, source, q_in, nk_in, nv_in, kbuf, vbuf, q3, nk, nv,
                  score, own, weight, own_weight, mixed, sems, ksem, vsem):
    rows, context = kbuf.shape[0], kbuf.shape[1]
    heads = q_in.shape[1] // HD
    group = rows // ksem.shape[0]

    def k_copy(i):
        part = pl.ds(i * group, group)
        return pltpu.make_async_copy(k_hbm.at[part], kbuf.at[part], ksem.at[i])

    def v_copy(i):
        part = pl.ds(i * group, group)
        return pltpu.make_async_copy(v_hbm.at[part], vbuf.at[part], vsem.at[i])

    small = [
        pltpu.make_async_copy(slot_hbm, slot, sems.at[0]),
        pltpu.make_async_copy(len_hbm, length, sems.at[1]),
        pltpu.make_async_copy(q_hbm, q_in, sems.at[2]),
        pltpu.make_async_copy(nk_hbm, nk_in, sems.at[3]),
        pltpu.make_async_copy(nv_hbm, nv_in, sems.at[4]),
    ]
    for copy in small:
        copy.start()
    for i in range(ksem.shape[0]):
        k_copy(i).start()
    for i in range(ksem.shape[0]):
        v_copy(i).start()
    for copy in small:
        copy.wait()
    for r in range(rows):
        source[lax.rem(slot[r], rows)] = r
    scale = HD ** (-0.5)
    for h in range(heads):
        q3[:, h, :] = q_in[:, h * HD : (h + 1) * HD].astype(F32)
    nk[...] = nk_in[...].astype(F32)
    nv[...] = nv_in[...].astype(F32)
    position = lax.broadcasted_iota(jnp.int32, (heads, context), 1)
    for i in range(ksem.shape[0]):
        k_copy(i).wait()
        for s in range(i * group, (i + 1) * group):
            r = source[s]
            q8 = q3[r]
            line = slice(s * heads, (s + 1) * heads)
            logits = dot(q8.astype(BF), kbuf[s], ((1,), (1,))) * scale
            score[line, :] = jnp.where(position < length[r], logits, MASKED)
            mine = jnp.sum(q8 * nk[pl.ds(r, 1), :], axis=1, keepdims=True) * scale
            own[line, :] = jnp.broadcast_to(mine, (heads, HD))
    logits = score[...]
    mine = own[:, 0:1]
    top = jnp.maximum(jnp.max(logits, axis=1, keepdims=True), mine)
    e = jnp.exp(logits - top)
    own_e = jnp.exp(mine - top)
    total = jnp.sum(e, axis=1, keepdims=True) + own_e
    weight[...] = (e / total).astype(BF)
    own_weight[...] = jnp.broadcast_to((own_e / total).astype(BF).astype(F32), own_weight.shape)
    for i in range(ksem.shape[0]):
        v_copy(i).wait()
        for s in range(i * group, (i + 1) * group):
            r = source[s]
            line = slice(s * heads, (s + 1) * heads)
            o = dot(weight[line, :], vbuf[s], ((1,), (0,)))
            mixed[r] = o + own_weight[line, :] * nv[pl.ds(r, 1), :]
    z0 = lax.axis_index("z0")
    for half in range(2):
        pairs = []
        for quarter in range(2):
            h = 4 * half + 2 * quarter
            pairs.append(jnp.concatenate([mixed[:, h, :], mixed[:, h + 1, :]], axis=1).astype(BF))
        first = jnp.where(z0 == 0, pairs[0], pairs[1])
        second = jnp.where(z0 == 0, pairs[1], pairs[0])
        value = jnp.concatenate([first, second], axis=1)
        for c in range(out_ref.shape[0]):
            out_ref[c, half] = value


def attend(copies, slots, lens, queries, new_keys, new_values, key_cache, value_cache):
    rows, context = key_cache.shape[0], key_cache.shape[1]
    heads = queries.shape[1] // HD
    chunks = 4
    hbm = pl.BlockSpec(memory_space=pltpu.HBM)
    return pl.pallas_call(
        attend_kernel,
        out_shape=jax.ShapeDtypeStruct((copies, 2, rows, heads // 2 * HD), BF),
        in_specs=[hbm] * 7,
        out_specs=pl.BlockSpec(memory_space=pltpu.VMEM),
        scratch_shapes=[
            pltpu.SMEM((rows,), jnp.int32),
            pltpu.SMEM((rows,), jnp.int32),
            pltpu.SMEM((rows,), jnp.int32),
            pltpu.VMEM(queries.shape, BF),
            pltpu.VMEM(new_keys.shape, BF),
            pltpu.VMEM(new_values.shape, BF),
            pltpu.VMEM((rows, context, HD), BF),
            pltpu.VMEM((rows, context, HD), BF),
            pltpu.VMEM((rows, heads, HD), F32),
            pltpu.VMEM((rows, HD), F32),
            pltpu.VMEM((rows, HD), F32),
            pltpu.VMEM((rows * heads, context), F32),
            pltpu.VMEM((rows * heads, HD), F32),
            pltpu.VMEM((rows * heads, context), BF),
            pltpu.VMEM((rows * heads, HD), F32),
            pltpu.VMEM((rows, heads, HD), F32),
            pltpu.SemaphoreType.DMA((5,)),
            pltpu.SemaphoreType.DMA((chunks,)),
            pltpu.SemaphoreType.DMA((chunks,)),
        ],
        compiler_params=pltpu.CompilerParams(vmem_limit_bytes=48 << 20),
        name="attend",
    )(*map(in_hbm, (slots, lens, queries, new_keys, new_values, key_cache, value_cache)))


def project_kernel(x_ref, w00, w01, w10, w11, out_ref):
    parts, rows = out_ref.shape[0], out_ref.shape[1]
    g = lax.axis_index("g")

    def stack(side):
        return jnp.concatenate([x_ref[p, side].astype(F32) for p in range(parts)], axis=0).astype(BF)

    mine, theirs = stack(g), stack(1 - g)
    half = w00.shape[0]
    total = dot(mine[:, :half], w00[...], ((1,), (0,)))
    total += dot(mine[:, half:], w01[...], ((1,), (0,)))
    total += dot(theirs[:, :half], w10[...], ((1,), (0,)))
    total += dot(theirs[:, half:], w11[...], ((1,), (0,)))
    out_ref[...] = total.reshape(parts, rows, total.shape[1]).astype(BF)


def project(x, weights):
    parts, _, rows, _ = x.shape
    vmem = pl.BlockSpec(memory_space=pltpu.VMEM)
    return pl.pallas_call(
        project_kernel,
        out_shape=jax.ShapeDtypeStruct((parts, rows, weights[0].shape[1]), BF),
        in_specs=[vmem] * 5,
        out_specs=vmem,
        compiler_params=pltpu.CompilerParams(vmem_limit_bytes=32 << 20),
        name="project",
    )(x, *weights)


def join_kernel(parts_ref, residual_ref, out_ref, copies_ref):
    total = residual_ref[...].astype(F32)
    acc = parts_ref[0].astype(F32)
    for p in range(1, parts_ref.shape[0]):
        acc += parts_ref[p].astype(F32)
    total = (total + acc).astype(BF)
    out_ref[...] = total
    for c in range(copies_ref.shape[0]):
        copies_ref[c] = total


def join(parts, residual, copies):
    vmem = pl.BlockSpec(memory_space=pltpu.VMEM)
    return pl.pallas_call(
        join_kernel,
        out_shape=(
            jax.ShapeDtypeStruct(residual.shape, BF),
            jax.ShapeDtypeStruct((copies, *residual.shape), BF),
        ),
        in_specs=[vmem, vmem],
        out_specs=(vmem, vmem),
        name="join",
    )(parts, residual)


TAIL = 16


def expand_kernel(first_ref, x_ref, wg_hbm, wu_hbm, *rest):
    u_hbm, wg, wu, held, staged, wsem, usem = rest[-7:]
    dests, height = staged.shape[0], staged.shape[1]
    per_dest = held.shape[0] // dests
    end = height - TAIL
    copies = [
        pltpu.make_async_copy(wg_hbm, wg, wsem.at[0]),
        pltpu.make_async_copy(wu_hbm, wu, wsem.at[1]),
    ]
    for copy in copies:
        copy.start()

    x = x_ref[...].astype(F32).reshape(held.shape)
    held[...] = x.astype(BF)
    folded = jnp.zeros((held.shape[0], HD), F32)
    for t in range(held.shape[1] // HD):
        v = x[:, t * HD : (t + 1) * HD]
        folded += v * v
    upper = folded.astype(BF)
    lower = (folded - upper.astype(F32)).astype(BF)
    ones = jnp.ones((TAIL, HD), BF)
    for d in range(dests):
        part = slice(d * per_dest, (d + 1) * per_dest)
        total = dot(ones, upper[part], ((1,), (1,))) + dot(ones, lower[part], ((1,), (1,)))
        top = total.astype(BF).astype(F32)
        line = lax.broadcasted_iota(jnp.int32, total.shape, 0)
        both = jnp.where(line == 0, top, jnp.where(line == 1, total - top, 0.0))
        staged[d, end:, :] = jnp.zeros((TAIL, HD), BF)
        staged[d, end:, 0:per_dest] = both.astype(BF)

    for w, copy, shift in ((wg, copies[0], 0), (wu, copies[1], per_dest)):
        copy.wait()
        for lane in range(0, w.shape[1], 2 * HD):
            width = min(2 * HD, w.shape[1] - lane)
            y = dot(held[...], w[:, lane : lane + width], ((1,), (0,))).astype(BF)
            for c in range(width // HD):
                row = (lane // HD + c) * 2 * per_dest + shift
                for d in range(dests):
                    staged[d, row : row + per_dest, :] = y[d * per_dest : (d + 1) * per_dest, c * HD : (c + 1) * HD]
    out = pltpu.make_async_copy(staged, u_hbm.at[pl.ds(first_ref[0] * dests, dests)], usem)
    out.start()
    out.wait()


def expand(first, x, wg, wu, so_far):
    parts, rows, depth = x.shape
    dests = 4
    per_dest = parts * rows // dests
    height = wg.shape[1] // HD * 2 * per_dest + TAIL
    hbm = pl.BlockSpec(memory_space=pltpu.HBM)
    specs = [pl.BlockSpec(memory_space=pltpu.SMEM), pl.BlockSpec(memory_space=pltpu.VMEM), hbm, hbm]
    args = [first, x, in_hbm(wg), in_hbm(wu)]
    aliases = {}
    if so_far is not None:
        specs.append(hbm)
        args.append(so_far)
        aliases = {4: 0}
    return pl.pallas_call(
        expand_kernel,
        out_shape=jax.ShapeDtypeStruct((8, height, HD), BF),
        in_specs=specs,
        out_specs=hbm,
        scratch_shapes=[
            pltpu.VMEM(wg.shape, BF),
            pltpu.VMEM(wu.shape, BF),
            pltpu.VMEM((parts * rows, depth), BF),
            pltpu.VMEM((dests, height, HD), BF),
            pltpu.SemaphoreType.DMA((2,)),
            pltpu.SemaphoreType.DMA,
        ],
        input_output_aliases=aliases,
        compiler_params=pltpu.CompilerParams(vmem_limit_bytes=32 << 20),
        name="expand",
    )(*args)


def activate_kernel(u_ref, out_ref):
    per_dest = out_ref.shape[0]
    end = u_ref.shape[1] - TAIL
    s = u_ref[0, end:, :].astype(F32)
    for p in range(1, u_ref.shape[0]):
        s += u_ref[p, end:, :].astype(F32)
    square = jnp.broadcast_to(s[0:1, :] + s[1:2, :], (HD, HD)).T
    scale = lax.rsqrt(square[:per_dest, :] / D + EPS)
    for c in range(end // (2 * per_dest)):
        start = c * 2 * per_dest
        total = u_ref[0, start : start + 2 * per_dest].astype(F32)
        for p in range(1, u_ref.shape[0]):
            total += u_ref[p, start : start + 2 * per_dest].astype(F32)
        gate = total[:per_dest] * scale
        up = total[per_dest:] * scale
        out_ref[:, c * HD : (c + 1) * HD] = (gate / (1.0 + jnp.exp(-gate)) * up).astype(BF)


def activate(u, per_dest):
    columns = (u.shape[1] - TAIL) // (2 * per_dest) * HD
    vmem = pl.BlockSpec(memory_space=pltpu.VMEM)
    return pl.pallas_call(
        activate_kernel,
        out_shape=jax.ShapeDtypeStruct((per_dest, columns), BF),
        in_specs=[vmem],
        out_specs=vmem,
        compiler_params=pltpu.CompilerParams(vmem_limit_bytes=32 << 20),
        name="activate",
    )(u)


def swapped(x, axis):
    return lax.ppermute(x, axis, [(0, 1), (1, 0)])


def exchange(x, axes):
    return lax.all_to_all(x, axes, 0, 0, tiled=True)


def scalar(*values):
    return jnp.stack([jnp.asarray(v, jnp.int32) for v in values])


def body(queries, new_keys, new_values, key_cache, value_cache, context_len, cache_slot,
         residual_in, out_weight, gate_weight, up_weight):
    rows = queries.shape[0]
    g = lax.axis_index("g")

    w01 = swapped(out_weight, "z0")
    w10 = swapped(out_weight, "g")
    w11 = swapped(w01, "g")

    attended = attend(8, cache_slot, context_len, queries, new_keys, new_values, key_cache, value_cache)
    attended, w10 = lax.optimization_barrier((attended, w10))
    heads = exchange(attended, MC)
    heads = heads.reshape(2, 4, *heads.shape[1:]).transpose(1, 2, 0, 3, 4)
    heads = heads.reshape(8, *heads.shape[2:])
    partial = project(exchange(heads, KAPPA), (out_weight, w01, w10, w11))
    residual_out, copies = join(exchange(partial, KAPPA), residual_in, 16)
    mine = exchange(copies, YLZ)
    theirs = swapped(mine, "g")
    u = expand(scalar(g), mine, gate_weight, up_weight, None)
    u = expand(scalar(1 - g), theirs, gate_weight, up_weight, u)
    activation = activate(exchange(u, MC), 4 * rows)
    return (residual_out, activation)


def solution(mesh):
    fine = Mesh(mesh.devices.reshape((2,) * 8), FINE)
    r = ("g",) + YLZ
    in_specs = (P(r, MC), P(r, MC), P(r, MC), P(r, None, MC), P(r, None, MC), P(r), P(r), P(r, MC),
                P(r, MC), P(MC, r), P(MC, r))
    out_specs = (P(r, MC), P(MC, r))
    return jax.shard_map(body, mesh=fine, in_specs=in_specs, out_specs=out_specs, check_vma=False)
```

time: 153 us -> 138 us (0.902)
  blocking collectives: 73.5 us -> 95.3 us
  starting transfers between devices: 35.8 us -> 15.7 us
  Pallas kernels: 28 us -> 16.4 us
  local copies, waits for them, and re-layouts: 7.14 us -> 0.79 us
  waiting for transfers between devices: 6.69 us -> 8.98 us
    all_to_all x3 -> x4, blocking collectives: 73.5 us -> 95.3 us  [exchange(): return lax.all_to_all(x, axes, 0, 0, tiled=True)]
    ppermute x2 -> x0, starting transfers between devices: 8.2 us -> none  [the longest x1 7.54 us: body(): half_b = lax.ppermute(half_b, FINE, partner_pairs(1))]
    all_to_all x1, starting transfers between devices: 15.3 us -> 7.4 us  [exchange(): return lax.all_to_all(x, axes, 0, 0, tiled=True)]
    unnamed x16 -> x2, local copies, waits for them, and re-layouts: 6.23 us -> 0.01 us
    pallas_call x4 -> x2, Pallas kernels: 12.2 us -> 7.7 us  [expand(): pl.pallas_call(expand_kernel, out_shape=jax.ShapeDtypeStruct((8, height,...]
    pallas_call x1, Pallas kernels: 5.21 us -> 1.14 us  [activate(): pl.pallas_call(activate_kernel, out_shape=jax.ShapeDtypeStruct((per_dest,...]
    ppermute x4, starting transfers between devices: 12.3 us -> 8.35 us  [swapped(): return lax.ppermute(x, axis, [(0, 1), (1, 0)])]
    pallas_call x2, Pallas kernels: 8.51 us -> 5.55 us  [the longest x1 4.96 us: attend(): pl.pallas_call(attend_kernel, out_shape=jax.ShapeDtypeStruct((copies, 2,...]
  transfers between devices with their start and end apart: 7 -> 5, of which waited for: 2 -> 2; matrix products, arithmetic and copies ran while one was open for 1% -> 1% of each run, Pallas kernels for 9% -> 6%
where the time goes in v2:
time: 138 us
  blocking collectives  95.3 us (69%)
  Pallas kernels  16.4 us (12%)
  starting transfers between devices  15.7 us (11%)
  waiting for transfers between devices  8.98 us (7%)
    all_to_all x4, blocking collectives, exchange(): return lax.all_to_all(x, axes, 0, 0, tiled=True)  95.3 us
    ppermute x4, starting transfers between devices, swapped(): return lax.ppermute(x, axis, [(0, 1), (1, 0)])  8.35 us
    pallas_call x2, Pallas kernels, expand(): pl.pallas_call(expand_kernel, out_shape=jax.ShapeDtypeStruct((8, height,...  7.7 us
    all_to_all x1, waiting for transfers between devices, exchange(): return lax.all_to_all(x, axes, 0, 0, tiled=True)  7.44 us
    all_to_all x1, starting transfers between devices, exchange(): return lax.all_to_all(x, axes, 0, 0, tiled=True)  7.4 us
    pallas_call x1, Pallas kernels, attend(): pl.pallas_call(attend_kernel, out_shape=jax.ShapeDtypeStruct((copies, 2,...  4.96 us
  transfers between devices with their start and end apart: 5, of which 2 were waited for; matrix products, arithmetic and copies ran while one was open for 1% of the time, Pallas kernels for 6%

profile of v2, /device:TPU:1, one launch (start us, length us, event | category | flops | bytes accessed | tf_op | source)
XLA Modules:
  0.0 137.8 jit_solution(13880654620312263617)
XLA Ops:
  0.6 0.0 copy-start
  0.6 3.3 %collective-permute-start = (bf16[256,1024]{1,0:T(8,128)(2,1)}, bf16[256,1024]{1,0:T(8,128)(2,1)S(1)}, u32[]{:S(2)}, u32[]{:S(2)}) collective-permute-start(bf16[256,1024]{1,0:T(8,128)(2,1)} %w00.1), channel_id=1, source_target_pairs={{0,128},{128,0},{1,129},{129,1},{2,130},{130,2},{3,131},{131,3},{4... | collective-permute-start | bytes 1572872 | tf_op jit(solution)/shard_map/ppermute | solution.py:309
  4.0 0.0 collective-permute-start.1
  4.0 5.0 %attend.1 = bf16[8,2,24,512]{3,2,1,0:T(8,128)(2,1)S(1)} custom-call(s32[24]{0:T(128)} %slot_hbm.1, s32[24]{0:T(128)} %len_hbm.1, bf16[24,1024]{1,0:T(8,128)(2,1)} %q_hbm.1, bf16[24,128]{1,0:T(8,128)(2,1)} %nk_hbm.1, bf16[24,128]{1,0:T(8,128)(2,1)} %nv_hbm.1, bf16[24,512,128]{2,1,0:T(8,128)(2,1)} %k_hbm.1, bf16[24,512,128]{2,1,0:T(8,128)(2,1)} %v_hbm.1), custom_call_target="tpu_custom_call" | custom-call | tf_op jit(solution)/shard_map/attend/pallas_call | solution.py:113
  8.9 0.0 collective-permute-done.w10
  9.0 16.3 %all_to_all.25 = bf16[8,2,24,512]{3,2,1,0:T(8,128)(2,1)S(1)} all-to-all(bf16[8,2,24,512]{3,2,1,0:T(8,128)(2,1)S(1)} %attend.1), channel_id=1, replica_groups=mesh['g'=2,'yl'=2,'zh'=2,'z1'=2,'z0'=2,'yh'=2,'xh'=2,'xl'=2] {'yh','xh',..., dimensions={0} | all-to-all | bytes 786432 | tf_op jit(solution)/shard_map/all_to_all | solution.py:313
  25.3 0.8 copy.14
  26.1 7.4 %all-to-all-start.1 = ((bf16[8,2,24,512]{3,2,1,0:T(8,128)(2,1)}), bf16[8,2,24,512]{3,2,1,0:T(8,128)(2,1)S(1)}, u32[]{:S(2)}, u32[]{:S(2)}) async-start(bf16[8,2,24,512]{3,2,1,0:T(8,128)(2,1)} %bitcast.2), calls=%async_computation.1 | async-start | bytes 786432 | tf_op jit(solution)/shard_map/all_to_all | solution.py:313
  33.5 0.0 collective-permute-done.1.w01
  33.5 1.5 %collective-permute-start.2 = (bf16[256,1024]{1,0:T(8,128)(2,1)S(1)}, bf16[256,1024]{1,0:T(8,128)(2,1)S(1)}, u32[]{:S(2)}, u32[]{:S(2)}) collective-permute-start(bf16[256,1024]{1,0:T(8,128)(2,1)S(1)} %collective-permute-done.1.w01), channel_id=1, source_target_pairs={{0,128},{128,0},{1,129},{129,1},{2,130},{130,2},{3,131},{131,3},{4... | collective-permute-start | bytes 1572872 | tf_op jit(solution)/shard_map/ppermute | solution.py:309
  35.0 1.5 %collective-permute-done.2.w11 = bf16[256,1024]{1,0:T(8,128)(2,1)S(1)} collective-permute-done((bf16[256,1024]{1,0:T(8,128)(2,1)S(1)}, bf16[256,1024]{1,0:T(8,128)(2,1)S(1)}, u32[]{:S(2)}, u32[]{:S(2)}) %collective-permute-start.2) | collective-permute-done | bytes 524320 | tf_op jit(solution)/shard_map/ppermute | solution.py:309
  36.6 7.4 %all-to-all-done.1.x_ref = bf16[8,2,24,512]{3,2,1,0:T(8,128)(2,1)S(1)} async-done(((bf16[8,2,24,512]{3,2,1,0:T(8,128)(2,1)}), bf16[8,2,24,512]{3,2,1,0:T(8,128)(2,1)S(1)}, u32[]{:S(2)}, u32[]{:S(2)}) %all-to-all-start.1) | async-done | bytes 393248 | tf_op jit(solution)/shard_map/all_to_all | solution.py:313
  44.0 0.0 copy-done
  44.0 0.6 project.1
  44.6 16.9 %all_to_all.26.parts_ref = bf16[8,24,1024]{2,1,0:T(8,128)(2,1)} all-to-all(bf16[8,24,1024]{2,1,0:T(8,128)(2,1)S(1)} %project.1), channel_id=1, replica_groups=mesh['g'=2,'yl'=2,'zh'=2,'z1'=2,'z0'=2,'yh'=2,'xh'=2,'xl'=2] {'yl','zh',..., dimensions={0} | all-to-all | bytes 786432 | tf_op jit(solution)/shard_map/all_to_all | solution.py:313
  61.5 2.0 %join.1 = (bf16[24,1024]{1,0:T(8,128)(2,1)}, bf16[16,24,1024]{2,1,0:T(8,128)(2,1)}) custom-call(bf16[8,24,1024]{2,1,0:T(8,128)(2,1)} %all_to_all.26.parts_ref, bf16[24,1024]{1,0:T(8,128)(2,1)} %residual_ref.1), custom_call_target="tpu_custom_call" | custom-call | tf_op jit(solution)/shard_map/join/pallas_call | solution.py:186
  63.5 23.7 %all_to_all.27.x_ref = bf16[16,24,1024]{2,1,0:T(8,128)(2,1)S(1)} all-to-all(bf16[16,24,1024]{2,1,0:T(8,128)(2,1)} %get-tuple-element.9), channel_id=1, replica_groups=mesh['g'=2,'yl'=2,'zh'=2,'z1'=2,'z0'=2,'yh'=2,'xh'=2,'xl'=2] {'yl','zh',..., dimensions={0} | all-to-all | bytes 1572864 | tf_op jit(solution)/shard_map/all_to_all | solution.py:313
  87.1 3.5 %collective-permute-start.3 = (bf16[16,24,1024]{2,1,0:T(8,128)(2,1)S(1)}, bf16[16,24,1024]{2,1,0:T(8,128)(2,1)S(1)}, u32[]{:S(2)}, u32[]{:S(2)}) collective-permute-start(bf16[16,24,1024]{2,1,0:T(8,128)(2,1)S(1)} %all_to_all.27.x_ref), channel_id=1, source_target_pairs={{0,128},{128,0},{1,129},{129,1},{2,130},{130,2},{3,131},{131,3},{4... | collective-permute-start | bytes 2359304 | tf_op jit(solution)/shard_map/ppermute | solution.py:309
  90.6 3.8 %expand.2.rest_0_ = bf16[8,1360,128]{2,1,0:T(8,128)(2,1)S(1)} custom-call(s32[1]{0:T(128)} %bitcast.4.first_ref, bf16[16,24,1024]{2,1,0:T(8,128)(2,1)S(1)} %all_to_all.27.x_ref, bf16[1024,896]{1,0:T(8,128)(2,1)} %wg_hbm.3, bf16[1024,896]{1,0:T(8,128)(2,1)} %wu_hbm.3), custom_call_target="tpu_custom_call" | custom-call | tf_op jit(solution)/shard_map/expand/pallas_call | solution.py:258
  94.5 0.0 collective-permute-done.3.x_ref
  94.5 3.8 %expand.3 = bf16[8,1360,128]{2,1,0:T(8,128)(2,1)S(1)} custom-call(s32[1]{0:T(128)} %bitcast.3.first_ref, bf16[16,24,1024]{2,1,0:T(8,128)(2,1)S(1)} %collective-permute-done.3.x_ref, bf16[1024,896]{1,0:T(8,128)(2,1)} %wg_hbm.3, bf16[1024,896]{1,0:T(8,128)(2,1)} %wu_hbm.3, bf16[8,1360,128]{2,1,0:T(8,128)(2,1)S(1)} %expand.2.rest_0_), custom_call_target="tpu_custom_call", output_to_operand_aliasing={{}: (4, {})} | custom-call | tf_op jit(solution)/shard_map/expand/pallas_call | solution.py:258
  98.3 38.3 %all_to_all.28.u_ref = bf16[8,1360,128]{2,1,0:T(8,128)(2,1)S(1)} all-to-all(bf16[8,1360,128]{2,1,0:T(8,128)(2,1)S(1)} %expand.3), channel_id=1, replica_groups=mesh['g'=2,'yl'=2,'zh'=2,'z1'=2,'z0'=2,'yh'=2,'xh'=2,'xl'=2] {'yh','xh',..., dimensions={0} | all-to-all | bytes 5570560 | tf_op jit(solution)/shard_map/all_to_all | solution.py:313
  136.7 1.1 activate.1
Async XLA Ops:
  0.6 43.4 %copy-start = (bf16[256,1024]{1,0:T(8,128)(2,1)S(1)}, bf16[256,1024]{1,0:T(8,128)(2,1)}, u32[]{:S(2)}) copy-start(bf16[256,1024]{1,0:T(8,128)(2,1)} %w00.1) | copy-start | bytes 1572868
  0.6 8.3 %collective-permute-start = (bf16[256,1024]{1,0:T(8,128)(2,1)}, bf16[256,1024]{1,0:T(8,128)(2,1)S(1)}, u32[]{:S(2)}, u32[]{:S(2)}) collective-permute-start(bf16[256,1024]{1,0:T(8,128)(2,1)} %w00.1), channel_id=1, source_target_pairs={{0,128},{128,0},{1,129},{129,1},{2,130},{130,2},{3,131},{131,3},{4... | collective-permute-start | bytes 1572872 | tf_op jit(solution)/shard_map/ppermute | solution.py:309
  4.0 29.5 %collective-permute-start.1 = (bf16[256,1024]{1,0:T(8,128)(2,1)}, bf16[256,1024]{1,0:T(8,128)(2,1)S(1)}, u32[]{:S(2)}, u32[]{:S(2)}) collective-permute-start(bf16[256,1024]{1,0:T(8,128)(2,1)} %w00.1), channel_id=1, source_target_pairs={{0,8},{8,0},{1,9},{9,1},{2,10},{10,2},{3,11},{11,3},{4,12},{12,4},... | collective-permute-start | bytes 1572872 | tf_op jit(solution)/shard_map/ppermute | solution.py:309
  26.1 17.9 %all-to-all-start.1 = ((bf16[8,2,24,512]{3,2,1,0:T(8,128)(2,1)}), bf16[8,2,24,512]{3,2,1,0:T(8,128)(2,1)S(1)}, u32[]{:S(2)}, u32[]{:S(2)}) async-start(bf16[8,2,24,512]{3,2,1,0:T(8,128)(2,1)} %bitcast.2), calls=%async_computation.1 | async-start | bytes 786432 | tf_op jit(solution)/shard_map/all_to_all | solution.py:313
  33.5 3.1 %collective-permute-start.2 = (bf16[256,1024]{1,0:T(8,128)(2,1)S(1)}, bf16[256,1024]{1,0:T(8,128)(2,1)S(1)}, u32[]{:S(2)}, u32[]{:S(2)}) collective-permute-start(bf16[256,1024]{1,0:T(8,128)(2,1)S(1)} %collective-permute-done.1.w01), channel_id=1, source_target_pairs={{0,128},{128,0},{1,129},{129,1},{2,130},{130,2},{3,131},{131,3},{4... | collective-permute-start | bytes 1572872 | tf_op jit(solution)/shard_map/ppermute | solution.py:309
  87.1 7.3 %collective-permute-start.3 = (bf16[16,24,1024]{2,1,0:T(8,128)(2,1)S(1)}, bf16[16,24,1024]{2,1,0:T(8,128)(2,1)S(1)}, u32[]{:S(2)}, u32[]{:S(2)}) collective-permute-start(bf16[16,24,1024]{2,1,0:T(8,128)(2,1)S(1)} %all_to_all.27.x_ref), channel_id=1, source_target_pairs={{0,128},{128,0},{1,129},{129,1},{2,130},{130,2},{3,131},{131,3},{4... | collective-permute-start | bytes 2359304 | tf_op jit(solution)/shard_map/ppermute | solution.py:309

commit v3 on v2

--- a/solution.py
+++ b/solution.py
@@ -55,8 +55,6 @@
         copy.start()
     for i in range(ksem.shape[0]):
         k_copy(i).start()
-    for i in range(ksem.shape[0]):
-        v_copy(i).start()
     for copy in small:
         copy.wait()
     for r in range(rows):
@@ -69,6 +67,7 @@
     position = lax.broadcasted_iota(jnp.int32, (heads, context), 1)
     for i in range(ksem.shape[0]):
         k_copy(i).wait()
+        v_copy(i).start()
         for s in range(i * group, (i + 1) * group):
             r = source[s]
             q8 = q3[r]
@@ -322,13 +321,12 @@
     rows = queries.shape[0]
     g = lax.axis_index("g")
 
+    attended = attend(8, cache_slot, context_len, queries, new_keys, new_values, key_cache, value_cache)
+    attended, out_weight = lax.optimization_barrier((attended, out_weight))
     w01 = swapped(out_weight, "z0")
-    w10 = swapped(out_weight, "g")
+    heads, w01, late = lax.optimization_barrier((exchange(attended, MC), w01, out_weight))
+    w10 = swapped(late, "g")
     w11 = swapped(w01, "g")
-
-    attended = attend(8, cache_slot, context_len, queries, new_keys, new_values, key_cache, value_cache)
-    attended, w10 = lax.optimization_barrier((attended, w10))
-    heads = exchange(attended, MC)
     heads = heads.reshape(2, 4, *heads.shape[1:]).transpose(1, 2, 0, 3, 4)
     heads = heads.reshape(8, *heads.shape[2:])
     partial = project(exchange(heads, KAPPA), (out_weight, w01, w10, w11))

time: 138 us -> 136 us (0.986)
  starting transfers between devices: 15.7 us -> 20.1 us
  blocking collectives: 95.3 us -> 91.8 us
  waiting for transfers between devices: 8.98 us -> 6.46 us
    ppermute x4, starting transfers between devices: 8.35 us -> 12.7 us  [swapped(): return lax.ppermute(x, axis, [(0, 1), (1, 0)])]
    all_to_all x4, blocking collectives: 95.3 us -> 91.8 us  [exchange(): return lax.all_to_all(x, axes, 0, 0, tiled=True)]
    all_to_all x1, waiting for transfers between devices: 7.44 us -> 4.26 us  [exchange(): return lax.all_to_all(x, axes, 0, 0, tiled=True)]
  transfers between devices with their start and end apart: 5 -> 5, of which waited for: 2 -> 3; matrix products, arithmetic and copies ran while one was open for 1% -> 0% of each run, Pallas kernels for 6% -> 3%
where the time goes in v3:
time: 136 us
  blocking collectives  91.8 us (68%)
  starting transfers between devices  20.1 us (15%)
  Pallas kernels  15.7 us (12%)
  waiting for transfers between devices  6.46 us (5%)
    all_to_all x4, blocking collectives, exchange(): return lax.all_to_all(x, axes, 0, 0, tiled=True)  91.8 us
    ppermute x4, starting transfers between devices, swapped(): return lax.ppermute(x, axis, [(0, 1), (1, 0)])  12.7 us
    pallas_call x2, Pallas kernels, expand(): pl.pallas_call(expand_kernel, out_shape=jax.ShapeDtypeStruct((8, height,...  7.7 us
    all_to_all x1, starting transfers between devices, exchange(): return lax.all_to_all(x, axes, 0, 0, tiled=True)  7.39 us
    pallas_call x1, Pallas kernels, attend(): pl.pallas_call(attend_kernel, out_shape=jax.ShapeDtypeStruct((copies, 2,...  4.31 us
    all_to_all x1, waiting for transfers between devices, exchange(): return lax.all_to_all(x, axes, 0, 0, tiled=True)  4.26 us
  transfers between devices with their start and end apart: 5, of which 3 were waited for; matrix products, arithmetic and copies ran while one was open for 0% of the time, Pallas kernels for 3%

profile of v3, /device:TPU:1, one launch (start us, length us, event | category | flops | bytes accessed | tf_op | source)
XLA Modules:
  0.0 135.6 jit_solution(6804026733468235218)
XLA Ops:
  0.6 0.0 copy-start
  0.6 4.3 %attend.1 = bf16[8,2,24,512]{3,2,1,0:T(8,128)(2,1)S(1)} custom-call(s32[24]{0:T(128)} %slot_hbm.1, s32[24]{0:T(128)} %len_hbm.1, bf16[24,1024]{1,0:T(8,128)(2,1)} %q_hbm.1, bf16[24,128]{1,0:T(8,128)(2,1)} %nk_hbm.1, bf16[24,128]{1,0:T(8,128)(2,1)} %nv_hbm.1, bf16[24,512,128]{2,1,0:T(8,128)(2,1)} %k_hbm.1, bf16[24,512,128]{2,1,0:T(8,128)(2,1)} %v_hbm.1), custom_call_target="tpu_custom_call" | custom-call | tf_op jit(solution)/shard_map/attend/pallas_call | solution.py:112
  5.0 0.0 copy-done
  5.0 2.6 %collective-permute-start = (bf16[256,1024]{1,0:T(8,128)(2,1)S(1)}, bf16[256,1024]{1,0:T(8,128)(2,1)S(1)}, u32[]{:S(2)}, u32[]{:S(2)}) collective-permute-start(bf16[256,1024]{1,0:T(8,128)(2,1)S(1)} %copy-done), channel_id=1, source_target_pairs={{0,8},{8,0},{1,9},{9,1},{2,10},{10,2},{3,11},{11,3},{4,12},{12,4},... | collective-permute-start | bytes 1572872 | tf_op jit(solution)/shard_map/ppermute | solution.py:308
  7.5 14.8 %all_to_all.25 = bf16[8,2,24,512]{3,2,1,0:T(8,128)(2,1)S(1)} all-to-all(bf16[8,2,24,512]{3,2,1,0:T(8,128)(2,1)S(1)} %attend.1), channel_id=1, replica_groups=mesh['g'=2,'yl'=2,'zh'=2,'z1'=2,'z0'=2,'yh'=2,'xh'=2,'xl'=2] {'yh','xh',..., dimensions={0} | all-to-all | bytes 786432 | tf_op jit(solution)/shard_map/all_to_all | solution.py:312
  22.4 0.0 collective-permute-done.w01
  22.4 0.8 copy.14
  23.1 7.4 %all-to-all-start.1 = ((bf16[8,2,24,512]{3,2,1,0:T(8,128)(2,1)}), bf16[8,2,24,512]{3,2,1,0:T(8,128)(2,1)S(1)}, u32[]{:S(2)}, u32[]{:S(2)}) async-start(bf16[8,2,24,512]{3,2,1,0:T(8,128)(2,1)} %bitcast.2), calls=%async_computation.1 | async-start | bytes 786432 | tf_op jit(solution)/shard_map/all_to_all | solution.py:312
  30.5 3.0 %collective-permute-start.1 = (bf16[256,1024]{1,0:T(8,128)(2,1)S(1)}, bf16[256,1024]{1,0:T(8,128)(2,1)S(1)}, u32[]{:S(2)}, u32[]{:S(2)}) collective-permute-start(bf16[256,1024]{1,0:T(8,128)(2,1)S(1)} %copy-done), channel_id=1, source_target_pairs={{0,128},{128,0},{1,129},{129,1},{2,130},{130,2},{3,131},{131,3},{4... | collective-permute-start | bytes 1572872 | tf_op jit(solution)/shard_map/ppermute | solution.py:308
  33.6 0.1 collective-permute-start.2
  33.7 1.4 %collective-permute-done.1.w10 = bf16[256,1024]{1,0:T(8,128)(2,1)S(1)} collective-permute-done((bf16[256,1024]{1,0:T(8,128)(2,1)S(1)}, bf16[256,1024]{1,0:T(8,128)(2,1)S(1)}, u32[]{:S(2)}, u32[]{:S(2)}) %collective-permute-start.1) | collective-permute-done | bytes 524320 | tf_op jit(solution)/shard_map/ppermute | solution.py:308
  35.1 0.7 collective-permute-done.2.w11
  35.9 4.3 %all-to-all-done.1.x_ref = bf16[8,2,24,512]{3,2,1,0:T(8,128)(2,1)S(1)} async-done(((bf16[8,2,24,512]{3,2,1,0:T(8,128)(2,1)}), bf16[8,2,24,512]{3,2,1,0:T(8,128)(2,1)S(1)}, u32[]{:S(2)}, u32[]{:S(2)}) %all-to-all-start.1) | async-done | bytes 393248 | tf_op jit(solution)/shard_map/all_to_all | solution.py:312
  40.1 0.6 project.1
  40.7 15.4 %all_to_all.26.parts_ref = bf16[8,24,1024]{2,1,0:T(8,128)(2,1)} all-to-all(bf16[8,24,1024]{2,1,0:T(8,128)(2,1)S(1)} %project.1), channel_id=1, replica_groups=mesh['g'=2,'yl'=2,'zh'=2,'z1'=2,'z0'=2,'yh'=2,'xh'=2,'xl'=2] {'yl','zh',..., dimensions={0} | all-to-all | bytes 786432 | tf_op jit(solution)/shard_map/all_to_all | solution.py:312
  56.1 2.0 %join.1 = (bf16[24,1024]{1,0:T(8,128)(2,1)}, bf16[16,24,1024]{2,1,0:T(8,128)(2,1)}) custom-call(bf16[8,24,1024]{2,1,0:T(8,128)(2,1)} %all_to_all.26.parts_ref, bf16[24,1024]{1,0:T(8,128)(2,1)} %residual_ref.1), custom_call_target="tpu_custom_call" | custom-call | tf_op jit(solution)/shard_map/join/pallas_call | solution.py:185
  58.1 19.6 %all_to_all.27.x_ref = bf16[16,24,1024]{2,1,0:T(8,128)(2,1)S(1)} all-to-all(bf16[16,24,1024]{2,1,0:T(8,128)(2,1)} %get-tuple-element.15), channel_id=1, replica_groups=mesh['g'=2,'yl'=2,'zh'=2,'z1'=2,'z0'=2,'yh'=2,'xh'=2,'xl'=2] {'yl','zh',..., dimensions={0} | all-to-all | bytes 1572864 | tf_op jit(solution)/shard_map/all_to_all | solution.py:312
  77.6 7.0 %collective-permute-start.3 = (bf16[16,24,1024]{2,1,0:T(8,128)(2,1)S(1)}, bf16[16,24,1024]{2,1,0:T(8,128)(2,1)S(1)}, u32[]{:S(2)}, u32[]{:S(2)}) collective-permute-start(bf16[16,24,1024]{2,1,0:T(8,128)(2,1)S(1)} %all_to_all.27.x_ref), channel_id=1, source_target_pairs={{0,128},{128,0},{1,129},{129,1},{2,130},{130,2},{3,131},{131,3},{4... | collective-permute-start | bytes 2359304 | tf_op jit(solution)/shard_map/ppermute | solution.py:308
  84.7 3.8 %expand.2.rest_0_ = bf16[8,1360,128]{2,1,0:T(8,128)(2,1)S(1)} custom-call(s32[1]{0:T(128)} %bitcast.4.first_ref, bf16[16,24,1024]{2,1,0:T(8,128)(2,1)S(1)} %all_to_all.27.x_ref, bf16[1024,896]{1,0:T(8,128)(2,1)} %wg_hbm.3, bf16[1024,896]{1,0:T(8,128)(2,1)} %wu_hbm.3), custom_call_target="tpu_custom_call" | custom-call | tf_op jit(solution)/shard_map/expand/pallas_call | solution.py:257
  88.5 0.0 collective-permute-done.3.x_ref
  88.5 3.9 %expand.3 = bf16[8,1360,128]{2,1,0:T(8,128)(2,1)S(1)} custom-call(s32[1]{0:T(128)} %bitcast.3.first_ref, bf16[16,24,1024]{2,1,0:T(8,128)(2,1)S(1)} %collective-permute-done.3.x_ref, bf16[1024,896]{1,0:T(8,128)(2,1)} %wg_hbm.3, bf16[1024,896]{1,0:T(8,128)(2,1)} %wu_hbm.3, bf16[8,1360,128]{2,1,0:T(8,128)(2,1)S(1)} %expand.2.rest_0_), custom_call_target="tpu_custom_call", output_to_operand_aliasing={{}: (4, {})} | custom-call | tf_op jit(solution)/shard_map/expand/pallas_call | solution.py:257
  92.4 42.1 %all_to_all.28.u_ref = bf16[8,1360,128]{2,1,0:T(8,128)(2,1)S(1)} all-to-all(bf16[8,1360,128]{2,1,0:T(8,128)(2,1)S(1)} %expand.3), channel_id=1, replica_groups=mesh['g'=2,'yl'=2,'zh'=2,'z1'=2,'z0'=2,'yh'=2,'xh'=2,'xl'=2] {'yh','xh',..., dimensions={0} | all-to-all | bytes 5570560 | tf_op jit(solution)/shard_map/all_to_all | solution.py:312
  134.5 1.1 activate.1
Async XLA Ops:
  0.6 4.3 %copy-start = (bf16[256,1024]{1,0:T(8,128)(2,1)S(1)}, bf16[256,1024]{1,0:T(8,128)(2,1)}, u32[]{:S(2)}) copy-start(bf16[256,1024]{1,0:T(8,128)(2,1)} %w00) | copy-start | bytes 1572868
  5.0 17.4 %collective-permute-start = (bf16[256,1024]{1,0:T(8,128)(2,1)S(1)}, bf16[256,1024]{1,0:T(8,128)(2,1)S(1)}, u32[]{:S(2)}, u32[]{:S(2)}) collective-permute-start(bf16[256,1024]{1,0:T(8,128)(2,1)S(1)} %copy-done), channel_id=1, source_target_pairs={{0,8},{8,0},{1,9},{9,1},{2,10},{10,2},{3,11},{11,3},{4,12},{12,4},... | collective-permute-start | bytes 1572872 | tf_op jit(solution)/shard_map/ppermute | solution.py:308
  23.1 17.0 %all-to-all-start.1 = ((bf16[8,2,24,512]{3,2,1,0:T(8,128)(2,1)}), bf16[8,2,24,512]{3,2,1,0:T(8,128)(2,1)S(1)}, u32[]{:S(2)}, u32[]{:S(2)}) async-start(bf16[8,2,24,512]{3,2,1,0:T(8,128)(2,1)} %bitcast.2), calls=%async_computation.1 | async-start | bytes 786432 | tf_op jit(solution)/shard_map/all_to_all | solution.py:312
  30.5 4.6 %collective-permute-start.1 = (bf16[256,1024]{1,0:T(8,128)(2,1)S(1)}, bf16[256,1024]{1,0:T(8,128)(2,1)S(1)}, u32[]{:S(2)}, u32[]{:S(2)}) collective-permute-start(bf16[256,1024]{1,0:T(8,128)(2,1)S(1)} %copy-done), channel_id=1, source_target_pairs={{0,128},{128,0},{1,129},{129,1},{2,130},{130,2},{3,131},{131,3},{4... | collective-permute-start | bytes 1572872 | tf_op jit(solution)/shard_map/ppermute | solution.py:308
  33.6 2.3 %collective-permute-start.2 = (bf16[256,1024]{1,0:T(8,128)(2,1)S(1)}, bf16[256,1024]{1,0:T(8,128)(2,1)S(1)}, u32[]{:S(2)}, u32[]{:S(2)}) collective-permute-start(bf16[256,1024]{1,0:T(8,128)(2,1)S(1)} %collective-permute-done.w01), channel_id=1, source_target_pairs={{0,128},{128,0},{1,129},{129,1},{2,130},{130,2},{3,131},{131,3},{4... | collective-permute-start | bytes 1572872 | tf_op jit(solution)/shard_map/ppermute | solution.py:308
  77.6 10.9 %collective-permute-start.3 = (bf16[16,24,1024]{2,1,0:T(8,128)(2,1)S(1)}, bf16[16,24,1024]{2,1,0:T(8,128)(2,1)S(1)}, u32[]{:S(2)}, u32[]{:S(2)}) collective-permute-start(bf16[16,24,1024]{2,1,0:T(8,128)(2,1)S(1)} %all_to_all.27.x_ref), channel_id=1, source_target_pairs={{0,128},{128,0},{1,129},{129,1},{2,130},{130,2},{3,131},{131,3},{4... | collective-permute-start | bytes 2359304 | tf_op jit(solution)/shard_map/ppermute | solution.py:308

commit v4 on v3

--- a/solution.py
+++ b/solution.py
@@ -198,47 +198,59 @@
 
 
 def expand_kernel(first_ref, x_ref, wg_hbm, wu_hbm, *rest):
-    u_hbm, wg, wu, held, staged, wsem, usem = rest[-7:]
+    u_hbm, wg, wu, held, squares, staged, wsem, usem = rest[-8:]
     dests, height = staged.shape[0], staged.shape[1]
     per_dest = held.shape[0] // dests
     end = height - TAIL
-    copies = [
+    parts, rows, depth = x_ref.shape
+    loads = [
         pltpu.make_async_copy(wg_hbm, wg, wsem.at[0]),
         pltpu.make_async_copy(wu_hbm, wu, wsem.at[1]),
     ]
-    for copy in copies:
-        copy.start()
-
-    x = x_ref[...].astype(F32).reshape(held.shape)
-    held[...] = x.astype(BF)
-    folded = jnp.zeros((held.shape[0], HD), F32)
-    for t in range(held.shape[1] // HD):
-        v = x[:, t * HD : (t + 1) * HD]
-        folded += v * v
-    upper = folded.astype(BF)
-    lower = (folded - upper.astype(F32)).astype(BF)
+    for load in loads:
+        load.start()
+
+    pair = 2 * rows
+    for p in range(parts // 2):
+        dest, half = p // 2, p % 2
+        first = 8 * (dest // 2) + dest % 2 + 4 * half
+        x = jnp.concatenate([x_ref[first].astype(F32), x_ref[first + 2].astype(F32)], axis=0)
+        part = slice(p * pair, (p + 1) * pair)
+        held[part, :] = x.astype(BF)
+        folded = x[:, :HD] * x[:, :HD]
+        for t in range(1, depth // HD):
+            v = x[:, t * HD : (t + 1) * HD]
+            folded += v * v
+        squares[part, :] = folded
     ones = jnp.ones((TAIL, HD), BF)
     for d in range(dests):
-        part = slice(d * per_dest, (d + 1) * per_dest)
-        total = dot(ones, upper[part], ((1,), (1,))) + dot(ones, lower[part], ((1,), (1,)))
+        v = squares[d * per_dest : (d + 1) * per_dest, :]
+        upper = v.astype(BF)
+        lower = (v - upper.astype(F32)).astype(BF)
+        total = dot(ones, upper, ((1,), (1,))) + dot(ones, lower, ((1,), (1,)))
         top = total.astype(BF).astype(F32)
         line = lax.broadcasted_iota(jnp.int32, total.shape, 0)
         both = jnp.where(line == 0, top, jnp.where(line == 1, total - top, 0.0))
         staged[d, end:, :] = jnp.zeros((TAIL, HD), BF)
         staged[d, end:, 0:per_dest] = both.astype(BF)
 
-    for w, copy, shift in ((wg, copies[0], 0), (wu, copies[1], per_dest)):
-        copy.wait()
+    to = pl.ds(first_ref[0] * dests, dests)
+    cuts = ((0, end // 2), (end // 2, end // 2 + TAIL))
+    outs = []
+    for k, w in enumerate((wg, wu)):
+        loads[k].wait()
         for lane in range(0, w.shape[1], 2 * HD):
             width = min(2 * HD, w.shape[1] - lane)
             y = dot(held[...], w[:, lane : lane + width], ((1,), (0,))).astype(BF)
             for c in range(width // HD):
-                row = (lane // HD + c) * 2 * per_dest + shift
+                row = k * (end // 2) + (lane // HD + c) * per_dest
                 for d in range(dests):
                     staged[d, row : row + per_dest, :] = y[d * per_dest : (d + 1) * per_dest, c * HD : (c + 1) * HD]
-    out = pltpu.make_async_copy(staged, u_hbm.at[pl.ds(first_ref[0] * dests, dests)], usem)
-    out.start()
-    out.wait()
+        cut = pl.ds(*cuts[k])
+        outs.append(pltpu.make_async_copy(staged.at[:, cut], u_hbm.at[to, cut], usem.at[k]))
+        outs[k].start()
+    for out in outs:
+        out.wait()
 
 
 def expand(first, x, wg, wu, so_far):
@@ -263,9 +275,10 @@
             pltpu.VMEM(wg.shape, BF),
             pltpu.VMEM(wu.shape, BF),
             pltpu.VMEM((parts * rows, depth), BF),
+            pltpu.VMEM((parts * rows, HD), F32),
             pltpu.VMEM((dests, height, HD), BF),
             pltpu.SemaphoreType.DMA((2,)),
-            pltpu.SemaphoreType.DMA,
+            pltpu.SemaphoreType.DMA((2,)),
         ],
         input_output_aliases=aliases,
         compiler_params=pltpu.CompilerParams(vmem_limit_bytes=32 << 20),
@@ -281,13 +294,15 @@
         s += u_ref[p, end:, :].astype(F32)
     square = jnp.broadcast_to(s[0:1, :] + s[1:2, :], (HD, HD)).T
     scale = lax.rsqrt(square[:per_dest, :] / D + EPS)
+    def added(start):
+        total = u_ref[0, start : start + per_dest].astype(F32)
+        for p in range(1, u_ref.shape[0]):
+            total += u_ref[p, start : start + per_dest].astype(F32)
+        return total * scale
+
     for c in range(end // (2 * per_dest)):
-        start = c * 2 * per_dest
-        total = u_ref[0, start : start + 2 * per_dest].astype(F32)
-        for p in range(1, u_ref.shape[0]):
-            total += u_ref[p, start : start + 2 * per_dest].astype(F32)
-        gate = total[:per_dest] * scale
-        up = total[per_dest:] * scale
+        gate = added(c * per_dest)
+        up = added(end // 2 + c * per_dest)
         out_ref[:, c * HD : (c + 1) * HD] = (gate / (1.0 + jnp.exp(-gate)) * up).astype(BF)
 
 
@@ -331,11 +346,11 @@
     heads = heads.reshape(8, *heads.shape[2:])
     partial = project(exchange(heads, KAPPA), (out_weight, w01, w10, w11))
     residual_out, copies = join(exchange(partial, KAPPA), residual_in, 16)
-    mine = exchange(copies, YLZ)
+    mine = exchange(copies, ("zh", "z1", "z0", "yl"))
     theirs = swapped(mine, "g")
     u = expand(scalar(g), mine, gate_weight, up_weight, None)
     u = expand(scalar(1 - g), theirs, gate_weight, up_weight, u)
-    activation = activate(exchange(u, MC), 4 * rows)
+    activation = activate(exchange(u, ("yh", "xl", "xh")), 4 * rows)
     return (residual_out, activation)
 
 

time: 136 us -> 138 us (1.015)
  blocking collectives: 91.8 us -> 94.5 us
    all_to_all x4, blocking collectives: 91.8 us -> 94.5 us  [exchange(): return lax.all_to_all(x, axes, 0, 0, tiled=True)]
where the time goes in v4:
time: 138 us; the launch traced here: 137 us
  blocking collectives  94.5 us (68%)
  starting transfers between devices  19.4 us (14%)
  Pallas kernels  15.6 us (11%)
  waiting for transfers between devices  6.46 us (5%)
    all_to_all x4, blocking collectives, exchange(): return lax.all_to_all(x, axes, 0, 0, tiled=True)  94.5 us
    ppermute x4, starting transfers between devices, swapped(): return lax.ppermute(x, axis, [(0, 1), (1, 0)])  12 us
    pallas_call x2, Pallas kernels, expand(): pl.pallas_call(expand_kernel, out_shape=jax.ShapeDtypeStruct((8, height,...  7.55 us
    all_to_all x1, starting transfers between devices, exchange(): return lax.all_to_all(x, axes, 0, 0, tiled=True)  7.39 us
    pallas_call x1, Pallas kernels, attend(): pl.pallas_call(attend_kernel, out_shape=jax.ShapeDtypeStruct((copies, 2,...  4.31 us
    all_to_all x1, waiting for transfers between devices, exchange(): return lax.all_to_all(x, axes, 0, 0, tiled=True)  4.26 us
  transfers between devices with their start and end apart: 5, of which 3 were waited for; matrix products, arithmetic and copies ran while one was open for 0% of the time, Pallas kernels for 3%

profile of v4, /device:TPU:1, one launch (start us, length us, event | category | flops | bytes accessed | tf_op | source)
XLA Modules:
  0.0 137.4 jit_solution(8478862947663853834)
XLA Ops:
  0.6 0.0 copy-start
  0.6 4.3 %attend.1 = bf16[8,2,24,512]{3,2,1,0:T(8,128)(2,1)S(1)} custom-call(s32[24]{0:T(128)} %slot_hbm.1, s32[24]{0:T(128)} %len_hbm.1, bf16[24,1024]{1,0:T(8,128)(2,1)} %q_hbm.1, bf16[24,128]{1,0:T(8,128)(2,1)} %nk_hbm.1, bf16[24,128]{1,0:T(8,128)(2,1)} %nv_hbm.1, bf16[24,512,128]{2,1,0:T(8,128)(2,1)} %k_hbm.1, bf16[24,512,128]{2,1,0:T(8,128)(2,1)} %v_hbm.1), custom_call_target="tpu_custom_call" | custom-call | tf_op jit(solution)/shard_map/attend/pallas_call | solution.py:112
  5.0 0.0 copy-done
  5.0 2.6 %collective-permute-start = (bf16[256,1024]{1,0:T(8,128)(2,1)S(1)}, bf16[256,1024]{1,0:T(8,128)(2,1)S(1)}, u32[]{:S(2)}, u32[]{:S(2)}) collective-permute-start(bf16[256,1024]{1,0:T(8,128)(2,1)S(1)} %copy-done), channel_id=1, source_target_pairs={{0,8},{8,0},{1,9},{9,1},{2,10},{10,2},{3,11},{11,3},{4,12},{12,4},... | collective-permute-start | bytes 1572872 | tf_op jit(solution)/shard_map/ppermute | solution.py:323
  7.5 14.8 %all_to_all.25 = bf16[8,2,24,512]{3,2,1,0:T(8,128)(2,1)S(1)} all-to-all(bf16[8,2,24,512]{3,2,1,0:T(8,128)(2,1)S(1)} %attend.1), channel_id=1, replica_groups=mesh['g'=2,'yl'=2,'zh'=2,'z1'=2,'z0'=2,'yh'=2,'xh'=2,'xl'=2] {'yh','xh',..., dimensions={0} | all-to-all | bytes 786432 | tf_op jit(solution)/shard_map/all_to_all | solution.py:327
  22.4 0.0 collective-permute-done.w01
  22.4 0.8 copy.14
  23.1 7.4 %all-to-all-start.1 = ((bf16[8,2,24,512]{3,2,1,0:T(8,128)(2,1)}), bf16[8,2,24,512]{3,2,1,0:T(8,128)(2,1)S(1)}, u32[]{:S(2)}, u32[]{:S(2)}) async-start(bf16[8,2,24,512]{3,2,1,0:T(8,128)(2,1)} %bitcast.2), calls=%async_computation.1 | async-start | bytes 786432 | tf_op jit(solution)/shard_map/all_to_all | solution.py:327
  30.5 3.0 %collective-permute-start.1 = (bf16[256,1024]{1,0:T(8,128)(2,1)S(1)}, bf16[256,1024]{1,0:T(8,128)(2,1)S(1)}, u32[]{:S(2)}, u32[]{:S(2)}) collective-permute-start(bf16[256,1024]{1,0:T(8,128)(2,1)S(1)} %copy-done), channel_id=1, source_target_pairs={{0,128},{128,0},{1,129},{129,1},{2,130},{130,2},{3,131},{131,3},{4... | collective-permute-start | bytes 1572872 | tf_op jit(solution)/shard_map/ppermute | solution.py:323
  33.6 0.1 collective-permute-start.2
  33.7 1.4 %collective-permute-done.1.w10 = bf16[256,1024]{1,0:T(8,128)(2,1)S(1)} collective-permute-done((bf16[256,1024]{1,0:T(8,128)(2,1)S(1)}, bf16[256,1024]{1,0:T(8,128)(2,1)S(1)}, u32[]{:S(2)}, u32[]{:S(2)}) %collective-permute-start.1) | collective-permute-done | bytes 524320 | tf_op jit(solution)/shard_map/ppermute | solution.py:323
  35.1 0.7 collective-permute-done.2.w11
  35.9 4.3 %all-to-all-done.1.x_ref = bf16[8,2,24,512]{3,2,1,0:T(8,128)(2,1)S(1)} async-done(((bf16[8,2,24,512]{3,2,1,0:T(8,128)(2,1)}), bf16[8,2,24,512]{3,2,1,0:T(8,128)(2,1)S(1)}, u32[]{:S(2)}, u32[]{:S(2)}) %all-to-all-start.1) | async-done | bytes 393248 | tf_op jit(solution)/shard_map/all_to_all | solution.py:327
  40.1 0.6 project.1
  40.7 15.4 %all_to_all.26.parts_ref = bf16[8,24,1024]{2,1,0:T(8,128)(2,1)} all-to-all(bf16[8,24,1024]{2,1,0:T(8,128)(2,1)S(1)} %project.1), channel_id=1, replica_groups=mesh['g'=2,'yl'=2,'zh'=2,'z1'=2,'z0'=2,'yh'=2,'xh'=2,'xl'=2] {'yl','zh',..., dimensions={0} | all-to-all | bytes 786432 | tf_op jit(solution)/shard_map/all_to_all | solution.py:327
  56.1 2.0 %join.1 = (bf16[24,1024]{1,0:T(8,128)(2,1)}, bf16[16,24,1024]{2,1,0:T(8,128)(2,1)}) custom-call(bf16[8,24,1024]{2,1,0:T(8,128)(2,1)} %all_to_all.26.parts_ref, bf16[24,1024]{1,0:T(8,128)(2,1)} %residual_ref.1), custom_call_target="tpu_custom_call" | custom-call | tf_op jit(solution)/shard_map/join/pallas_call | solution.py:185
  58.1 22.2 %all_to_all.27.x_ref = bf16[16,24,1024]{2,1,0:T(8,128)(2,1)S(1)} all-to-all(bf16[16,24,1024]{2,1,0:T(8,128)(2,1)} %get-tuple-element.15), channel_id=1, replica_groups=mesh['g'=2,'yl'=2,'zh'=2,'z1'=2,'z0'=2,'yh'=2,'xh'=2,'xl'=2] {'zh','z1',..., dimensions={0} | all-to-all | bytes 1572864 | tf_op jit(solution)/shard_map/all_to_all | solution.py:327
  80.3 6.4 %collective-permute-start.3 = (bf16[16,24,1024]{2,1,0:T(8,128)(2,1)S(1)}, bf16[16,24,1024]{2,1,0:T(8,128)(2,1)S(1)}, u32[]{:S(2)}, u32[]{:S(2)}) collective-permute-start(bf16[16,24,1024]{2,1,0:T(8,128)(2,1)S(1)} %all_to_all.27.x_ref), channel_id=1, source_target_pairs={{0,128},{128,0},{1,129},{129,1},{2,130},{130,2},{3,131},{131,3},{4... | collective-permute-start | bytes 2359304 | tf_op jit(solution)/shard_map/ppermute | solution.py:323
  86.6 3.8 %expand.2.rest_0_ = bf16[8,1360,128]{2,1,0:T(8,128)(2,1)S(1)} custom-call(s32[1]{0:T(128)} %bitcast.4.first_ref, bf16[16,24,1024]{2,1,0:T(8,128)(2,1)S(1)} %all_to_all.27.x_ref, bf16[1024,896]{1,0:T(8,128)(2,1)} %wg_hbm.3, bf16[1024,896]{1,0:T(8,128)(2,1)} %wu_hbm.3), custom_call_target="tpu_custom_call" | custom-call | tf_op jit(solution)/shard_map/expand/pallas_call | solution.py:269
  90.4 0.0 collective-permute-done.3.x_ref
  90.4 3.8 %expand.3 = bf16[8,1360,128]{2,1,0:T(8,128)(2,1)S(1)} custom-call(s32[1]{0:T(128)} %bitcast.3.first_ref, bf16[16,24,1024]{2,1,0:T(8,128)(2,1)S(1)} %collective-permute-done.3.x_ref, bf16[1024,896]{1,0:T(8,128)(2,1)} %wg_hbm.3, bf16[1024,896]{1,0:T(8,128)(2,1)} %wu_hbm.3, bf16[8,1360,128]{2,1,0:T(8,128)(2,1)S(1)} %expand.2.rest_0_), custom_call_target="tpu_custom_call", output_to_operand_aliasing={{}: (4, {})} | custom-call | tf_op jit(solution)/shard_map/expand/pallas_call | solution.py:269
  94.2 42.1 %all_to_all.28.u_ref = bf16[8,1360,128]{2,1,0:T(8,128)(2,1)S(1)} all-to-all(bf16[8,1360,128]{2,1,0:T(8,128)(2,1)S(1)} %expand.3), channel_id=1, replica_groups=mesh['g'=2,'yl'=2,'zh'=2,'z1'=2,'z0'=2,'yh'=2,'xh'=2,'xl'=2] {'yh','xl',..., dimensions={0} | all-to-all | bytes 5570560 | tf_op jit(solution)/shard_map/all_to_all | solution.py:327
  136.3 1.1 activate.1
Async XLA Ops:
  0.6 4.3 %copy-start = (bf16[256,1024]{1,0:T(8,128)(2,1)S(1)}, bf16[256,1024]{1,0:T(8,128)(2,1)}, u32[]{:S(2)}) copy-start(bf16[256,1024]{1,0:T(8,128)(2,1)} %w00) | copy-start | bytes 1572868
  5.0 17.4 %collective-permute-start = (bf16[256,1024]{1,0:T(8,128)(2,1)S(1)}, bf16[256,1024]{1,0:T(8,128)(2,1)S(1)}, u32[]{:S(2)}, u32[]{:S(2)}) collective-permute-start(bf16[256,1024]{1,0:T(8,128)(2,1)S(1)} %copy-done), channel_id=1, source_target_pairs={{0,8},{8,0},{1,9},{9,1},{2,10},{10,2},{3,11},{11,3},{4,12},{12,4},... | collective-permute-start | bytes 1572872 | tf_op jit(solution)/shard_map/ppermute | solution.py:323
  23.1 17.0 %all-to-all-start.1 = ((bf16[8,2,24,512]{3,2,1,0:T(8,128)(2,1)}), bf16[8,2,24,512]{3,2,1,0:T(8,128)(2,1)S(1)}, u32[]{:S(2)}, u32[]{:S(2)}) async-start(bf16[8,2,24,512]{3,2,1,0:T(8,128)(2,1)} %bitcast.2), calls=%async_computation.1 | async-start | bytes 786432 | tf_op jit(solution)/shard_map/all_to_all | solution.py:327
  30.5 4.6 %collective-permute-start.1 = (bf16[256,1024]{1,0:T(8,128)(2,1)S(1)}, bf16[256,1024]{1,0:T(8,128)(2,1)S(1)}, u32[]{:S(2)}, u32[]{:S(2)}) collective-permute-start(bf16[256,1024]{1,0:T(8,128)(2,1)S(1)} %copy-done), channel_id=1, source_target_pairs={{0,128},{128,0},{1,129},{129,1},{2,130},{130,2},{3,131},{131,3},{4... | collective-permute-start | bytes 1572872 | tf_op jit(solution)/shard_map/ppermute | solution.py:323
  33.6 2.3 %collective-permute-start.2 = (bf16[256,1024]{1,0:T(8,128)(2,1)S(1)}, bf16[256,1024]{1,0:T(8,128)(2,1)S(1)}, u32[]{:S(2)}, u32[]{:S(2)}) collective-permute-start(bf16[256,1024]{1,0:T(8,128)(2,1)S(1)} %collective-permute-done.w01), channel_id=1, source_target_pairs={{0,128},{128,0},{1,129},{129,1},{2,130},{130,2},{3,131},{131,3},{4... | collective-permute-start | bytes 1572872 | tf_op jit(solution)/shard_map/ppermute | solution.py:323
  80.3 10.1 %collective-permute-start.3 = (bf16[16,24,1024]{2,1,0:T(8,128)(2,1)S(1)}, bf16[16,24,1024]{2,1,0:T(8,128)(2,1)S(1)}, u32[]{:S(2)}, u32[]{:S(2)}) collective-permute-start(bf16[16,24,1024]{2,1,0:T(8,128)(2,1)S(1)} %all_to_all.27.x_ref), channel_id=1, source_target_pairs={{0,128},{128,0},{1,129},{129,1},{2,130},{130,2},{3,131},{131,3},{4... | collective-permute-start | bytes 2359304 | tf_op jit(solution)/shard_map/ppermute | solution.py:323
